TPU v7x, 32 devices: a whole 2x2x4 slice. The times are simulated.
32 devices in a mesh: groups: 2 (over x), ctx: 16 (over z, y, core).
Axes of the slice: x: 2, y: 2, z: 4, core: 2. Of those that a mesh axis runs over, the one named last changes fastest.
Arguments:
- q_in: bfloat16 [8192, 4096], P(('groups', 'ctx')), parts along dimension 0, may hold values from -6 to 6
- k_in: bfloat16 [8192, 4096], P(('groups', 'ctx')), parts along dimension 0, may hold values from -6 to 6
- v_in: bfloat16 [8192, 4096], P(('groups', 'ctx')), parts along dimension 0, may hold values from -6 to 6
- conv_filter: float32 [3, 7, 4096], replicated, may hold values from -2 to 2
- decay_rate: float32 [256, 16], replicated, may hold values from 2.4414063e-05 to 0.133333333, as said below
- residue: float32 [256, 16], replicated, may hold values from -0.387298335 to 0.387298335
- genome_lengths: int32 [8], P('groups'), parts along dimension 0, may hold values from 1 to 2048, as said below
Outputs:
- gated: bfloat16 [8192, 4096], P(('groups', 'ctx')), parts along dimension 0
There are 2 independent parts, one for each index of `groups`. A program takes and returns all parts, laid end to end along the dimension named above; an argument that names none is the same for every part. Nothing has to cross between parts.
Inputs may be any that keep to these rules, and one draw needn't show every extreme that they name: `decay_rate`: positive rates. `genome_lengths`: positive lengths that sum to 4096; one genome holds exactly 2048 bases.
All inputs are finite; a program needn't handle non-finite values.
Results may differ from a plain program's by a relative error of at most 0.0065.
Values may be sent and summed in bfloat16 or wider, within the bound.
No kernel may reach another device: no remote copies, remote signals or barrier semaphores. Data moves between devices by JAX's collectives and lax.ppermute only.
A program may use at most 128 MiB of HBM per device.

v0:
```python
import math

import jax
import jax.numpy as jnp
from jax import lax
from jax.sharding import PartitionSpec as P

CPG = 16
POLES = 16
TAPS = 7


def shifted(value, axis, steps):
    count = lax.axis_size(axis)
    leading, last = (max(0, -steps), min(count, count - steps))
    return lax.ppermute(value, axis, [(source, source + steps) for source in range(leading, last)])


def segment_ids(genome_lengths, positions):
    starts = jnp.cumsum(genome_lengths) - genome_lengths
    return jnp.sum((starts[None, :] <= positions[:, None]).astype(jnp.int32), axis=1)


def per_device(q_in, k_in, v_in, conv_filter, decay_rate, residue, genome_lengths):
    row_count = q_in.shape[0]
    width = q_in.shape[1]
    filter_count = width // CPG
    reach = TAPS - 1
    device_index = lax.axis_index("ctx")
    first_row = device_index * row_count
    positions = first_row + jnp.arange(row_count, dtype=jnp.int32)
    segments = segment_ids(genome_lengths, positions)
    tail_ids = segment_ids(genome_lengths, first_row - reach + jnp.arange(reach, dtype=jnp.int32))
    prior_id = segment_ids(genome_lengths, jnp.reshape(first_row - 1, (1,)))[0]
    streams = jnp.stack([q_in, k_in, v_in])
    tail_block = shifted(streams[:, row_count - reach :], "ctx", 1)
    extended = jnp.concatenate([tail_block, streams], axis=1)
    extended_ids = jnp.concatenate([tail_ids, segments])
    featured = jnp.zeros((3, row_count, width), jnp.float32)
    for offset_tap in range(TAPS):
        lower = reach - offset_tap
        window = extended[:, lower : lower + row_count].astype(jnp.float32)
        keep = (extended_ids[lower : lower + row_count] == segments).astype(jnp.float32)
        featured = featured + conv_filter[:, offset_tap][:, None, :] * window * keep[None, :, None]
    featured = featured.astype(jnp.bfloat16)
    query = featured[0]
    mixed = featured[1].astype(jnp.float32) * featured[2].astype(jnp.float32)
    mixed_filters = mixed.reshape(row_count, filter_count, CPG)
    rate_t = decay_rate.T
    offsets = jnp.arange(row_count, dtype=jnp.float32)
    centered = offsets - 0.5 * row_count
    left_factor = residue[:, :, None] * jnp.exp(-decay_rate[:, :, None] * centered[None, None, :])
    right_factor = jnp.exp(decay_rate[:, :, None] * centered[None, None, :])
    row_idx = jnp.arange(row_count, dtype=jnp.int32)
    causal_mask = (
        (row_idx[:, None] >= row_idx[None, :]) & (segments[:, None] == segments[None, :])
    ).astype(jnp.float32)
    block_filters = math.gcd(filter_count, 32)
    block_total = filter_count // block_filters

    def local_block(block_id):
        left_rows = lax.dynamic_slice_in_dim(
            left_factor, block_id * block_filters, block_filters, 0
        )
        right_rows = lax.dynamic_slice_in_dim(
            right_factor, block_id * block_filters, block_filters, 0
        )
        toeplitz = (
            jnp.einsum("gnt,gns->gts", left_rows, right_rows, precision=lax.Precision.HIGHEST)
            * causal_mask[None]
        )
        inputs_block = lax.dynamic_slice_in_dim(
            mixed_filters, block_id * block_filters, block_filters, 1
        )
        return jnp.einsum("gts,sgc->tgc", toeplitz, inputs_block, precision=lax.Precision.HIGHEST)

    local_parts = lax.map(local_block, jnp.arange(block_total, dtype=jnp.int32))
    local_out = jnp.transpose(local_parts, (1, 0, 2, 3)).reshape(row_count, width)
    end_keep = (segments == segments[row_count - 1]).astype(jnp.float32)
    end_powers = (
        jnp.exp(-rate_t[None] * (row_count - 1.0 - offsets)[:, None, None])
        * end_keep[:, None, None]
    )
    span_state = jnp.einsum(
        "tng,tgc->ngc", end_powers, mixed_filters, precision=lax.Precision.HIGHEST
    ).reshape(POLES, width)
    carries_on = (segments[row_count - 1] == prior_id).astype(jnp.float32)
    span_decay = jnp.exp(-rate_t * row_count) * carries_on

    def pass_on(turn, incoming):
        outgoing = (span_decay[:, :, None] * incoming.reshape(POLES, filter_count, CPG)).reshape(
            POLES, width
        ) + span_state
        return shifted(outgoing, "ctx", 1)

    incoming = lax.fori_loop(
        0, lax.axis_size("ctx") - 1, pass_on, jnp.zeros((POLES, width), jnp.float32)
    )
    start_keep = (segments == prior_id).astype(jnp.float32)
    start_powers = jnp.exp(-rate_t[None] * (offsets + 1.0)[:, None, None])
    start_powers = start_powers * residue.T[None] * start_keep[:, None, None]
    carried_out = jnp.einsum(
        "tng,ngc->tgc",
        start_powers,
        incoming.reshape(POLES, filter_count, CPG),
        precision=lax.Precision.HIGHEST,
    ).reshape(row_count, width)
    filtered = local_out + carried_out
    return (query.astype(jnp.float32) * filtered).astype(jnp.bfloat16)


def solution(mesh):
    in_specs = (
        P(("groups", "ctx"), None),
        P(("groups", "ctx"), None),
        P(("groups", "ctx"), None),
        P(),
        P(),
        P(),
        P("groups"),
    )
    out_specs = P(("groups", "ctx"), None)
    return jax.shard_map(
        per_device, mesh=mesh, in_specs=in_specs, out_specs=out_specs, check_vma=False
    )
```

profile of v0, /device:TPU:18, one launch (start us, length us, event | category | flops | bytes accessed | tf_op | source)
XLA Modules:
  0.0 407.6 jit_solution(13818663312346447885)
XLA Ops:
  37.1 9.5 %maximum_maximum_fusion = bf16[3,262,4096]{1,2,0:T(8,128)(2,1)S(1)} fusion(bf16[1,256,4096]{1,2,0:T(8,128)(2,1)} %bitcast.69, bf16[1,256,4096]{1,2,0:T(8,128)(2,1)} %bitcast.66, bf16[1,256,4096]{1,2,0:T(8,128)(2,1)S(1)} %bitcast.63, bf16[3,6,4096]{1,2,0:T(8,128)(2,1)} %copy.47), kind=kLoop, calls=%fused_computation.17 | loop fusion | flops 25755648 | bytes 12877824 | tf_op jit(solution)/shard_map/concatenate | solution.py:37
  46.6 28.3 %add_convert_fusion = bf16[3,256,4096]{1,2,0:T(8,128)(2,1)S(1)} fusion(bf16[3,262,4096]{1,2,0:T(8,128)(2,1)S(1)} %maximum_maximum_fusion, f32[256]{0:T(256)S(1)} %copy-done.12, f32[3,4096]{1,0:T(4,128)S(1)} %get-tuple-element.155, f32[256]{0:T(256)S(1)} %copy-done.11, f32[3,4096]{1,0:T(4,128)S(1)} %get-tuple-element.156, f32[256]{0:T(256)S(1)} %copy-done.10, ...), kind=kLoop, calls=%fused_computation.16 | loop fusion | flops 91226112 | bytes 50681856 | tf_op jit(solution)/shard_map/convert_element_type | solution.py:45
  80.1 146.8 %while.22 = (s32[]{:T(128)}, f32[8,256,32,16]{1,3,2,0:T(8,128)}, s32[8]{0:T(128)S(1)}, f32[256,256,16]{0,2,1:T(8,128)}, f32[256,16,256]{2,1,0:T(8,128)}, /*index...) while((s32[]{:T(128)}, f32[8,256,32,16]{1,3,2,0:T(8,128)}, ...), condition=%wide.region_4.5_spmd.clone, body=%wide.region_3.4_spmd.clone.sunk | while | flops 807665664 | bytes 19401388 | solution.py:77
  81.3 8.0 %fusion.53 = f32[32,256,256]{2,1,0:T(8,128)S(1)} fusion(f32[256,16,256]{2,1,0:T(8,128)} %get-tuple-element.271, s32[]{:T(128)S(6)} %select_n.7, f32[256,16,256]{2,1,0:T(8,128)} %get-tuple-element.270), kind=kOutput, calls=%fused_computation.7.clone.1 | convolution fusion | flops 402653184 | bytes 9438208 | tf_op jit(solution)/shard_map/while/body/eval_jaxpr/gnt,gns->gts/dot_general | solution.py:69
  89.4 9.0 %fusion.55 = f32[8,256,32,16]{1,3,2,0:T(8,128)} fusion(f32[8,256,32,16]{1,3,2,0:T(8,128)} %get-tuple-element.256, s32[]{:T(128)} %get-tuple-element.255, f32[32,256,256]{2,1,0:T(8,128)S(1)} %fusion.53, f32[256,256]{1,0:T(8,128)S(1)} %fusion.54, f32[256,256,16]{0,2,1:T(8,128)} %get-tuple-element.269, s32[]{:T(128)S(6)} %select_n.7), kind=kOutput, calls=%fused_computation.6.clone.1 | convolution fusion | flops 404750336 | bytes 9699844 | tf_op jit(solution)/shard_map/while/body/eval_jaxpr/gts,sgc->tgc/dot_general | solution.py:75
  99.7 8.0 %fusion.53 = f32[32,256,256]{2,1,0:T(8,128)S(1)} fusion(f32[256,16,256]{2,1,0:T(8,128)} %get-tuple-element.271, s32[]{:T(128)S(6)} %select_n.7, f32[256,16,256]{2,1,0:T(8,128)} %get-tuple-element.270), kind=kOutput, calls=%fused_computation.7.clone.1 | convolution fusion | flops 402653184 | bytes 9438208 | tf_op jit(solution)/shard_map/while/body/eval_jaxpr/gnt,gns->gts/dot_general | solution.py:69
  107.8 9.0 %fusion.55 = f32[8,256,32,16]{1,3,2,0:T(8,128)} fusion(f32[8,256,32,16]{1,3,2,0:T(8,128)} %get-tuple-element.256, s32[]{:T(128)} %get-tuple-element.255, f32[32,256,256]{2,1,0:T(8,128)S(1)} %fusion.53, f32[256,256]{1,0:T(8,128)S(1)} %fusion.54, f32[256,256,16]{0,2,1:T(8,128)} %get-tuple-element.269, s32[]{:T(128)S(6)} %select_n.7), kind=kOutput, calls=%fused_computation.6.clone.1 | convolution fusion | flops 404750336 | bytes 9699844 | tf_op jit(solution)/shard_map/while/body/eval_jaxpr/gts,sgc->tgc/dot_general | solution.py:75
  118.0 8.0 %fusion.53 = f32[32,256,256]{2,1,0:T(8,128)S(1)} fusion(f32[256,16,256]{2,1,0:T(8,128)} %get-tuple-element.271, s32[]{:T(128)S(6)} %select_n.7, f32[256,16,256]{2,1,0:T(8,128)} %get-tuple-element.270), kind=kOutput, calls=%fused_computation.7.clone.1 | convolution fusion | flops 402653184 | bytes 9438208 | tf_op jit(solution)/shard_map/while/body/eval_jaxpr/gnt,gns->gts/dot_general | solution.py:69
  126.1 9.0 %fusion.55 = f32[8,256,32,16]{1,3,2,0:T(8,128)} fusion(f32[8,256,32,16]{1,3,2,0:T(8,128)} %get-tuple-element.256, s32[]{:T(128)} %get-tuple-element.255, f32[32,256,256]{2,1,0:T(8,128)S(1)} %fusion.53, f32[256,256]{1,0:T(8,128)S(1)} %fusion.54, f32[256,256,16]{0,2,1:T(8,128)} %get-tuple-element.269, s32[]{:T(128)S(6)} %select_n.7), kind=kOutput, calls=%fused_computation.6.clone.1 | convolution fusion | flops 404750336 | bytes 9699844 | tf_op jit(solution)/shard_map/while/body/eval_jaxpr/gts,sgc->tgc/dot_general | solution.py:75
  136.3 8.0 %fusion.53 = f32[32,256,256]{2,1,0:T(8,128)S(1)} fusion(f32[256,16,256]{2,1,0:T(8,128)} %get-tuple-element.271, s32[]{:T(128)S(6)} %select_n.7, f32[256,16,256]{2,1,0:T(8,128)} %get-tuple-element.270), kind=kOutput, calls=%fused_computation.7.clone.1 | convolution fusion | flops 402653184 | bytes 9438208 | tf_op jit(solution)/shard_map/while/body/eval_jaxpr/gnt,gns->gts/dot_general | solution.py:69
  144.5 9.0 %fusion.55 = f32[8,256,32,16]{1,3,2,0:T(8,128)} fusion(f32[8,256,32,16]{1,3,2,0:T(8,128)} %get-tuple-element.256, s32[]{:T(128)} %get-tuple-element.255, f32[32,256,256]{2,1,0:T(8,128)S(1)} %fusion.53, f32[256,256]{1,0:T(8,128)S(1)} %fusion.54, f32[256,256,16]{0,2,1:T(8,128)} %get-tuple-element.269, s32[]{:T(128)S(6)} %select_n.7), kind=kOutput, calls=%fused_computation.6.clone.1 | convolution fusion | flops 404750336 | bytes 9699844 | tf_op jit(solution)/shard_map/while/body/eval_jaxpr/gts,sgc->tgc/dot_general | solution.py:75
  154.7 8.0 %fusion.53 = f32[32,256,256]{2,1,0:T(8,128)S(1)} fusion(f32[256,16,256]{2,1,0:T(8,128)} %get-tuple-element.271, s32[]{:T(128)S(6)} %select_n.7, f32[256,16,256]{2,1,0:T(8,128)} %get-tuple-element.270), kind=kOutput, calls=%fused_computation.7.clone.1 | convolution fusion | flops 402653184 | bytes 9438208 | tf_op jit(solution)/shard_map/while/body/eval_jaxpr/gnt,gns->gts/dot_general | solution.py:69
  162.8 9.0 %fusion.55 = f32[8,256,32,16]{1,3,2,0:T(8,128)} fusion(f32[8,256,32,16]{1,3,2,0:T(8,128)} %get-tuple-element.256, s32[]{:T(128)} %get-tuple-element.255, f32[32,256,256]{2,1,0:T(8,128)S(1)} %fusion.53, f32[256,256]{1,0:T(8,128)S(1)} %fusion.54, f32[256,256,16]{0,2,1:T(8,128)} %get-tuple-element.269, s32[]{:T(128)S(6)} %select_n.7), kind=kOutput, calls=%fused_computation.6.clone.1 | convolution fusion | flops 404750336 | bytes 9699844 | tf_op jit(solution)/shard_map/while/body/eval_jaxpr/gts,sgc->tgc/dot_general | solution.py:75
  173.0 8.0 %fusion.53 = f32[32,256,256]{2,1,0:T(8,128)S(1)} fusion(f32[256,16,256]{2,1,0:T(8,128)} %get-tuple-element.271, s32[]{:T(128)S(6)} %select_n.7, f32[256,16,256]{2,1,0:T(8,128)} %get-tuple-element.270), kind=kOutput, calls=%fused_computation.7.clone.1 | convolution fusion | flops 402653184 | bytes 9438208 | tf_op jit(solution)/shard_map/while/body/eval_jaxpr/gnt,gns->gts/dot_general | solution.py:69
  181.1 9.0 %fusion.55 = f32[8,256,32,16]{1,3,2,0:T(8,128)} fusion(f32[8,256,32,16]{1,3,2,0:T(8,128)} %get-tuple-element.256, s32[]{:T(128)} %get-tuple-element.255, f32[32,256,256]{2,1,0:T(8,128)S(1)} %fusion.53, f32[256,256]{1,0:T(8,128)S(1)} %fusion.54, f32[256,256,16]{0,2,1:T(8,128)} %get-tuple-element.269, s32[]{:T(128)S(6)} %select_n.7), kind=kOutput, calls=%fused_computation.6.clone.1 | convolution fusion | flops 404750336 | bytes 9699844 | tf_op jit(solution)/shard_map/while/body/eval_jaxpr/gts,sgc->tgc/dot_general | solution.py:75
  191.4 8.0 %fusion.53 = f32[32,256,256]{2,1,0:T(8,128)S(1)} fusion(f32[256,16,256]{2,1,0:T(8,128)} %get-tuple-element.271, s32[]{:T(128)S(6)} %select_n.7, f32[256,16,256]{2,1,0:T(8,128)} %get-tuple-element.270), kind=kOutput, calls=%fused_computation.7.clone.1 | convolution fusion | flops 402653184 | bytes 9438208 | tf_op jit(solution)/shard_map/while/body/eval_jaxpr/gnt,gns->gts/dot_general | solution.py:69
  199.5 9.0 %fusion.55 = f32[8,256,32,16]{1,3,2,0:T(8,128)} fusion(f32[8,256,32,16]{1,3,2,0:T(8,128)} %get-tuple-element.256, s32[]{:T(128)} %get-tuple-element.255, f32[32,256,256]{2,1,0:T(8,128)S(1)} %fusion.53, f32[256,256]{1,0:T(8,128)S(1)} %fusion.54, f32[256,256,16]{0,2,1:T(8,128)} %get-tuple-element.269, s32[]{:T(128)S(6)} %select_n.7), kind=kOutput, calls=%fused_computation.6.clone.1 | convolution fusion | flops 404750336 | bytes 9699844 | tf_op jit(solution)/shard_map/while/body/eval_jaxpr/gts,sgc->tgc/dot_general | solution.py:75
  209.7 8.0 %fusion.53 = f32[32,256,256]{2,1,0:T(8,128)S(1)} fusion(f32[256,16,256]{2,1,0:T(8,128)} %get-tuple-element.271, s32[]{:T(128)S(6)} %select_n.7, f32[256,16,256]{2,1,0:T(8,128)} %get-tuple-element.270), kind=kOutput, calls=%fused_computation.7.clone.1 | convolution fusion | flops 402653184 | bytes 9438208 | tf_op jit(solution)/shard_map/while/body/eval_jaxpr/gnt,gns->gts/dot_general | solution.py:69
  217.8 9.0 %fusion.55 = f32[8,256,32,16]{1,3,2,0:T(8,128)} fusion(f32[8,256,32,16]{1,3,2,0:T(8,128)} %get-tuple-element.256, s32[]{:T(128)} %get-tuple-element.255, f32[32,256,256]{2,1,0:T(8,128)S(1)} %fusion.53, f32[256,256]{1,0:T(8,128)S(1)} %fusion.54, f32[256,256,16]{0,2,1:T(8,128)} %get-tuple-element.269, s32[]{:T(128)S(6)} %select_n.7), kind=kOutput, calls=%fused_computation.6.clone.1 | convolution fusion | flops 404750336 | bytes 9699844 | tf_op jit(solution)/shard_map/while/body/eval_jaxpr/gts,sgc->tgc/dot_general | solution.py:75
  233.8 161.9 %while.21 = (s32[]{:T(128)}, f32[16,4096]{1,0:T(8,128)S(1)}, f32[16,256]{1,0:T(8,128)S(1)}, f32[16,4096]{1,0:T(8,128)S(1)}, s32[]{:T(128)}) while((s32[]{:T(128)}, f32[16,4096]{1,0:T(8,128)S(1)}, f32[16,256]{1,0:T(8,128)S(1)}, f32[16,4096]{1,0:T(8,128)S(1)}, s32[]{:T(128)}) %tuple.63), condition=%wide.region_7.8_spmd, body=%wide.region_6.7_spmd.sunk | while | flops 131074 | bytes 2900069 | solution.py:96
  248.7 6.7 %collective-permute-done = f32[16,4096]{1,0:T(8,128)S(1)} collective-permute-done((f32[16,4096]{1,0:T(8,128)S(1)}, f32[16,4096]{1,0:T(8,128)S(1)}, u32[]{:S(2)}, u32[]{:S(2)}) %collective-permute-start) | collective-permute-done | bytes 262176 | tf_op jit(solution)/shard_map/while/body/eval_jaxpr/ppermute | solution.py:16
  259.5 6.7 %collective-permute-done = f32[16,4096]{1,0:T(8,128)S(1)} collective-permute-done((f32[16,4096]{1,0:T(8,128)S(1)}, f32[16,4096]{1,0:T(8,128)S(1)}, u32[]{:S(2)}, u32[]{:S(2)}) %collective-permute-start) | collective-permute-done | bytes 262176 | tf_op jit(solution)/shard_map/while/body/eval_jaxpr/ppermute | solution.py:16
  270.3 6.7 %collective-permute-done = f32[16,4096]{1,0:T(8,128)S(1)} collective-permute-done((f32[16,4096]{1,0:T(8,128)S(1)}, f32[16,4096]{1,0:T(8,128)S(1)}, u32[]{:S(2)}, u32[]{:S(2)}) %collective-permute-start) | collective-permute-done | bytes 262176 | tf_op jit(solution)/shard_map/while/body/eval_jaxpr/ppermute | solution.py:16
  281.1 6.7 %collective-permute-done = f32[16,4096]{1,0:T(8,128)S(1)} collective-permute-done((f32[16,4096]{1,0:T(8,128)S(1)}, f32[16,4096]{1,0:T(8,128)S(1)}, u32[]{:S(2)}, u32[]{:S(2)}) %collective-permute-start) | collective-permute-done | bytes 262176 | tf_op jit(solution)/shard_map/while/body/eval_jaxpr/ppermute | solution.py:16
  291.9 6.7 %collective-permute-done = f32[16,4096]{1,0:T(8,128)S(1)} collective-permute-done((f32[16,4096]{1,0:T(8,128)S(1)}, f32[16,4096]{1,0:T(8,128)S(1)}, u32[]{:S(2)}, u32[]{:S(2)}) %collective-permute-start) | collective-permute-done | bytes 262176 | tf_op jit(solution)/shard_map/while/body/eval_jaxpr/ppermute | solution.py:16
  302.7 6.7 %collective-permute-done = f32[16,4096]{1,0:T(8,128)S(1)} collective-permute-done((f32[16,4096]{1,0:T(8,128)S(1)}, f32[16,4096]{1,0:T(8,128)S(1)}, u32[]{:S(2)}, u32[]{:S(2)}) %collective-permute-start) | collective-permute-done | bytes 262176 | tf_op jit(solution)/shard_map/while/body/eval_jaxpr/ppermute | solution.py:16
  313.5 6.7 %collective-permute-done = f32[16,4096]{1,0:T(8,128)S(1)} collective-permute-done((f32[16,4096]{1,0:T(8,128)S(1)}, f32[16,4096]{1,0:T(8,128)S(1)}, u32[]{:S(2)}, u32[]{:S(2)}) %collective-permute-start) | collective-permute-done | bytes 262176 | tf_op jit(solution)/shard_map/while/body/eval_jaxpr/ppermute | solution.py:16
  324.3 6.7 %collective-permute-done = f32[16,4096]{1,0:T(8,128)S(1)} collective-permute-done((f32[16,4096]{1,0:T(8,128)S(1)}, f32[16,4096]{1,0:T(8,128)S(1)}, u32[]{:S(2)}, u32[]{:S(2)}) %collective-permute-start) | collective-permute-done | bytes 262176 | tf_op jit(solution)/shard_map/while/body/eval_jaxpr/ppermute | solution.py:16
  335.1 6.7 %collective-permute-done = f32[16,4096]{1,0:T(8,128)S(1)} collective-permute-done((f32[16,4096]{1,0:T(8,128)S(1)}, f32[16,4096]{1,0:T(8,128)S(1)}, u32[]{:S(2)}, u32[]{:S(2)}) %collective-permute-start) | collective-permute-done | bytes 262176 | tf_op jit(solution)/shard_map/while/body/eval_jaxpr/ppermute | solution.py:16
  345.8 6.7 %collective-permute-done = f32[16,4096]{1,0:T(8,128)S(1)} collective-permute-done((f32[16,4096]{1,0:T(8,128)S(1)}, f32[16,4096]{1,0:T(8,128)S(1)}, u32[]{:S(2)}, u32[]{:S(2)}) %collective-permute-start) | collective-permute-done | bytes 262176 | tf_op jit(solution)/shard_map/while/body/eval_jaxpr/ppermute | solution.py:16
  356.6 6.7 %collective-permute-done = f32[16,4096]{1,0:T(8,128)S(1)} collective-permute-done((f32[16,4096]{1,0:T(8,128)S(1)}, f32[16,4096]{1,0:T(8,128)S(1)}, u32[]{:S(2)}, u32[]{:S(2)}) %collective-permute-start) | collective-permute-done | bytes 262176 | tf_op jit(solution)/shard_map/while/body/eval_jaxpr/ppermute | solution.py:16
  378.2 6.7 %collective-permute-done = f32[16,4096]{1,0:T(8,128)S(1)} collective-permute-done((f32[16,4096]{1,0:T(8,128)S(1)}, f32[16,4096]{1,0:T(8,128)S(1)}, u32[]{:S(2)}, u32[]{:S(2)}) %collective-permute-start) | collective-permute-done | bytes 262176 | tf_op jit(solution)/shard_map/while/body/eval_jaxpr/ppermute | solution.py:16
  (159 shorter events, 146.5 us)
Async XLA Ops:
  14.6 7.7 %copy-start.6 = (f32[256,16]{0,1:T(8,128)S(1)}, f32[256,16]{0,1:T(8,128)}, u32[]{:S(2)}) copy-start(f32[256,16]{0,1:T(8,128)} %param.15) | copy-start | bytes 49156
  14.6 7.9 %copy-start.17 = (s32[4]{0:T(128)S(1)}, s32[4]{0:T(128)}, u32[]{:S(2)}) copy-start(s32[4]{0:T(128)} %param.17) | copy-start | bytes 52
  14.6 13.0 %copy-start.3 = (f32[3,7,4096]{2,1,0:T(8,128)S(1)}, f32[3,7,4096]{2,1,0:T(8,128)}, u32[]{:S(2)}) copy-start(f32[3,7,4096]{2,1,0:T(8,128)} %param.14) | copy-start | bytes 1032196
  14.6 13.4 %copy-start.7 = (f32[256,16]{0,1:T(8,128)S(1)}, f32[256,16]{0,1:T(8,128)}, u32[]{:S(2)}) copy-start(f32[256,16]{0,1:T(8,128)} %param.16) | copy-start | bytes 49156
  20.4 13.8 %collective-permute-start.1 = (bf16[3,6,4096]{2,1,0:T(8,128)(2,1)S(1)}, bf16[3,6,4096]{2,1,0:T(8,128)(2,1)S(1)}, u32[]{:S(2)}, u32[]{:S(2)}) collective-permute-start(bf16[3,6,4096]{2,1,0:T(8,128)(2,1)S(1)} %copy.46), channel_id=1, source_target_pairs={{0,1},{1,2},{2,3},{3,4},{4,5},{5,6},{6,7},{7,8},{8,9},{9,10},{10,1... | collective-permute-start | bytes 442376 | tf_op jit(solution)/shard_map/ppermute | solution.py:16
  37.0 9.5 %copy-start = (bf16[256,4096]{0,1:T(8,128)(2,1)S(1)}, bf16[256,4096]{0,1:T(8,128)(2,1)}, u32[]{:S(2)}) copy-start(bf16[256,4096]{0,1:T(8,128)(2,1)} %copy.44) | copy-start | bytes 6291460
  37.0 9.5 %copy-start.1 = (bf16[256,4096]{0,1:T(8,128)(2,1)S(1)}, bf16[256,4096]{0,1:T(8,128)(2,1)}, u32[]{:S(2)}) copy-start(bf16[256,4096]{0,1:T(8,128)(2,1)} %copy.45) | copy-start | bytes 6291460
  37.0 9.5 %copy-start.8 = (f32[256]{0:T(256)S(1)}, f32[256]{0:T(256)}, u32[]{:S(2)}) copy-start(f32[256]{0:T(256)} %get-tuple-element.149) | copy-start | bytes 3076
  37.0 9.6 %copy-start.9 = (f32[256]{0:T(256)S(1)}, f32[256]{0:T(256)}, u32[]{:S(2)}) copy-start(f32[256]{0:T(256)} %get-tuple-element.150) | copy-start | bytes 3076
  37.0 9.6 %copy-start.10 = (f32[256]{0:T(256)S(1)}, f32[256]{0:T(256)}, u32[]{:S(2)}) copy-start(f32[256]{0:T(256)} %get-tuple-element.151) | copy-start | bytes 3076
  37.1 9.6 %copy-start.11 = (f32[256]{0:T(256)S(1)}, f32[256]{0:T(256)}, u32[]{:S(2)}) copy-start(f32[256]{0:T(256)} %get-tuple-element.152) | copy-start | bytes 3076
  37.1 9.6 %copy-start.12 = (f32[256]{0:T(256)S(1)}, f32[256]{0:T(256)}, u32[]{:S(2)}) copy-start(f32[256]{0:T(256)} %get-tuple-element.153) | copy-start | bytes 3076
  37.1 9.6 %copy-start.13 = (f32[256]{0:T(256)S(1)}, f32[256]{0:T(256)}, u32[]{:S(2)}) copy-start(f32[256]{0:T(256)} %get-tuple-element.154) | copy-start | bytes 3076
  75.0 2.7 copy-start.2
  80.1 146.8 %copy-start.15 = (f32[256]{0:T(256)S(1)}, f32[256]{0:T(256)}, u32[]{:S(2)}) copy-start(f32[256]{0:T(256)} %get-tuple-element.148) | copy-start | bytes 3076
  233.7 162.6 %copy-start.14 = (f32[256]{0:T(256)S(1)}, f32[256]{0:T(256)}, u32[]{:S(2)}) copy-start(f32[256]{0:T(256)} %get-tuple-element.147) | copy-start | bytes 3076
  233.7 162.6 %copy-start.16 = (f32[256]{0:T(256)S(1)}, f32[256]{0:T(256)}, u32[]{:S(2)}) copy-start(f32[256]{0:T(256)} %iota_add_fusion) | copy-start | bytes 3076
  236.0 8.6 %collective-permute-start = (f32[16,4096]{1,0:T(8,128)S(1)}, f32[16,4096]{1,0:T(8,128)S(1)}, u32[]{:S(2)}, u32[]{:S(2)}) collective-permute-start(f32[16,4096]{1,0:T(8,128)S(1)} %multiply_add_fusion.2), channel_id=1, source_target_pairs={{0,1},{1,2},{2,3},{3,4},{4,5},{5,6},{6,7},{7,8},{8,9},{9,10},{10,1... | collective-permute-start | bytes 786440 | tf_op jit(solution)/shard_map/while/body/eval_jaxpr/ppermute | solution.py:16
  246.8 8.6 %collective-permute-start = (f32[16,4096]{1,0:T(8,128)S(1)}, f32[16,4096]{1,0:T(8,128)S(1)}, u32[]{:S(2)}, u32[]{:S(2)}) collective-permute-start(f32[16,4096]{1,0:T(8,128)S(1)} %multiply_add_fusion.2), channel_id=1, source_target_pairs={{0,1},{1,2},{2,3},{3,4},{4,5},{5,6},{6,7},{7,8},{8,9},{9,10},{10,1... | collective-permute-start | bytes 786440 | tf_op jit(solution)/shard_map/while/body/eval_jaxpr/ppermute | solution.py:16
  257.6 8.6 %collective-permute-start = (f32[16,4096]{1,0:T(8,128)S(1)}, f32[16,4096]{1,0:T(8,128)S(1)}, u32[]{:S(2)}, u32[]{:S(2)}) collective-permute-start(f32[16,4096]{1,0:T(8,128)S(1)} %multiply_add_fusion.2), channel_id=1, source_target_pairs={{0,1},{1,2},{2,3},{3,4},{4,5},{5,6},{6,7},{7,8},{8,9},{9,10},{10,1... | collective-permute-start | bytes 786440 | tf_op jit(solution)/shard_map/while/body/eval_jaxpr/ppermute | solution.py:16
  268.4 8.6 %collective-permute-start = (f32[16,4096]{1,0:T(8,128)S(1)}, f32[16,4096]{1,0:T(8,128)S(1)}, u32[]{:S(2)}, u32[]{:S(2)}) collective-permute-start(f32[16,4096]{1,0:T(8,128)S(1)} %multiply_add_fusion.2), channel_id=1, source_target_pairs={{0,1},{1,2},{2,3},{3,4},{4,5},{5,6},{6,7},{7,8},{8,9},{9,10},{10,1... | collective-permute-start | bytes 786440 | tf_op jit(solution)/shard_map/while/body/eval_jaxpr/ppermute | solution.py:16
  279.1 8.6 %collective-permute-start = (f32[16,4096]{1,0:T(8,128)S(1)}, f32[16,4096]{1,0:T(8,128)S(1)}, u32[]{:S(2)}, u32[]{:S(2)}) collective-permute-start(f32[16,4096]{1,0:T(8,128)S(1)} %multiply_add_fusion.2), channel_id=1, source_target_pairs={{0,1},{1,2},{2,3},{3,4},{4,5},{5,6},{6,7},{7,8},{8,9},{9,10},{10,1... | collective-permute-start | bytes 786440 | tf_op jit(solution)/shard_map/while/body/eval_jaxpr/ppermute | solution.py:16
  289.9 8.6 %collective-permute-start = (f32[16,4096]{1,0:T(8,128)S(1)}, f32[16,4096]{1,0:T(8,128)S(1)}, u32[]{:S(2)}, u32[]{:S(2)}) collective-permute-start(f32[16,4096]{1,0:T(8,128)S(1)} %multiply_add_fusion.2), channel_id=1, source_target_pairs={{0,1},{1,2},{2,3},{3,4},{4,5},{5,6},{6,7},{7,8},{8,9},{9,10},{10,1... | collective-permute-start | bytes 786440 | tf_op jit(solution)/shard_map/while/body/eval_jaxpr/ppermute | solution.py:16
  300.7 8.6 %collective-permute-start = (f32[16,4096]{1,0:T(8,128)S(1)}, f32[16,4096]{1,0:T(8,128)S(1)}, u32[]{:S(2)}, u32[]{:S(2)}) collective-permute-start(f32[16,4096]{1,0:T(8,128)S(1)} %multiply_add_fusion.2), channel_id=1, source_target_pairs={{0,1},{1,2},{2,3},{3,4},{4,5},{5,6},{6,7},{7,8},{8,9},{9,10},{10,1... | collective-permute-start | bytes 786440 | tf_op jit(solution)/shard_map/while/body/eval_jaxpr/ppermute | solution.py:16
  311.5 8.6 %collective-permute-start = (f32[16,4096]{1,0:T(8,128)S(1)}, f32[16,4096]{1,0:T(8,128)S(1)}, u32[]{:S(2)}, u32[]{:S(2)}) collective-permute-start(f32[16,4096]{1,0:T(8,128)S(1)} %multiply_add_fusion.2), channel_id=1, source_target_pairs={{0,1},{1,2},{2,3},{3,4},{4,5},{5,6},{6,7},{7,8},{8,9},{9,10},{10,1... | collective-permute-start | bytes 786440 | tf_op jit(solution)/shard_map/while/body/eval_jaxpr/ppermute | solution.py:16
  322.3 8.6 %collective-permute-start = (f32[16,4096]{1,0:T(8,128)S(1)}, f32[16,4096]{1,0:T(8,128)S(1)}, u32[]{:S(2)}, u32[]{:S(2)}) collective-permute-start(f32[16,4096]{1,0:T(8,128)S(1)} %multiply_add_fusion.2), channel_id=1, source_target_pairs={{0,1},{1,2},{2,3},{3,4},{4,5},{5,6},{6,7},{7,8},{8,9},{9,10},{10,1... | collective-permute-start | bytes 786440 | tf_op jit(solution)/shard_map/while/body/eval_jaxpr/ppermute | solution.py:16
  333.1 8.6 %collective-permute-start = (f32[16,4096]{1,0:T(8,128)S(1)}, f32[16,4096]{1,0:T(8,128)S(1)}, u32[]{:S(2)}, u32[]{:S(2)}) collective-permute-start(f32[16,4096]{1,0:T(8,128)S(1)} %multiply_add_fusion.2), channel_id=1, source_target_pairs={{0,1},{1,2},{2,3},{3,4},{4,5},{5,6},{6,7},{7,8},{8,9},{9,10},{10,1... | collective-permute-start | bytes 786440 | tf_op jit(solution)/shard_map/while/body/eval_jaxpr/ppermute | solution.py:16
  343.9 8.6 %collective-permute-start = (f32[16,4096]{1,0:T(8,128)S(1)}, f32[16,4096]{1,0:T(8,128)S(1)}, u32[]{:S(2)}, u32[]{:S(2)}) collective-permute-start(f32[16,4096]{1,0:T(8,128)S(1)} %multiply_add_fusion.2), channel_id=1, source_target_pairs={{0,1},{1,2},{2,3},{3,4},{4,5},{5,6},{6,7},{7,8},{8,9},{9,10},{10,1... | collective-permute-start | bytes 786440 | tf_op jit(solution)/shard_map/while/body/eval_jaxpr/ppermute | solution.py:16
  354.7 8.6 %collective-permute-start = (f32[16,4096]{1,0:T(8,128)S(1)}, f32[16,4096]{1,0:T(8,128)S(1)}, u32[]{:S(2)}, u32[]{:S(2)}) collective-permute-start(f32[16,4096]{1,0:T(8,128)S(1)} %multiply_add_fusion.2), channel_id=1, source_target_pairs={{0,1},{1,2},{2,3},{3,4},{4,5},{5,6},{6,7},{7,8},{8,9},{9,10},{10,1... | collective-permute-start | bytes 786440 | tf_op jit(solution)/shard_map/while/body/eval_jaxpr/ppermute | solution.py:16
  365.5 8.6 %collective-permute-start = (f32[16,4096]{1,0:T(8,128)S(1)}, f32[16,4096]{1,0:T(8,128)S(1)}, u32[]{:S(2)}, u32[]{:S(2)}) collective-permute-start(f32[16,4096]{1,0:T(8,128)S(1)} %multiply_add_fusion.2), channel_id=1, source_target_pairs={{0,1},{1,2},{2,3},{3,4},{4,5},{5,6},{6,7},{7,8},{8,9},{9,10},{10,1... | collective-permute-start | bytes 786440 | tf_op jit(solution)/shard_map/while/body/eval_jaxpr/ppermute | solution.py:16
  376.3 8.6 %collective-permute-start = (f32[16,4096]{1,0:T(8,128)S(1)}, f32[16,4096]{1,0:T(8,128)S(1)}, u32[]{:S(2)}, u32[]{:S(2)}) collective-permute-start(f32[16,4096]{1,0:T(8,128)S(1)} %multiply_add_fusion.2), channel_id=1, source_target_pairs={{0,1},{1,2},{2,3},{3,4},{4,5},{5,6},{6,7},{7,8},{8,9},{9,10},{10,1... | collective-permute-start | bytes 786440 | tf_op jit(solution)/shard_map/while/body/eval_jaxpr/ppermute | solution.py:16
  387.1 8.6 %collective-permute-start = (f32[16,4096]{1,0:T(8,128)S(1)}, f32[16,4096]{1,0:T(8,128)S(1)}, u32[]{:S(2)}, u32[]{:S(2)}) collective-permute-start(f32[16,4096]{1,0:T(8,128)S(1)} %multiply_add_fusion.2), channel_id=1, source_target_pairs={{0,1},{1,2},{2,3},{3,4},{4,5},{5,6},{6,7},{7,8},{8,9},{9,10},{10,1... | collective-permute-start | bytes 786440 | tf_op jit(solution)/shard_map/while/body/eval_jaxpr/ppermute | solution.py:16
  (2 other events, 4.6 us)
where the time goes:
time: 409 us; the launch traced here: 408 us
  matrix products  147 us (36%)
  waiting for transfers between devices  98.3 us (24%)
  local copies, waits for them, and re-layouts  66.2 us (16%)
  other arithmetic  56.6 us (14%)
  starting transfers between devices  32.3 us (8%)
  loops' own time  5.75 us (1%)
    ppermute x16, waiting for transfers between devices, shifted(): lax.ppermute(value, axis, [(source, source + steps) for source in range(l...  98.3 us
    dot_general x8, matrix products, local_block(): jnp.einsum('gts,sgc->tgc', toeplitz, inputs_block, precision=lax.Precisio...  72 us
    dot_general x8, matrix products, local_block(): jnp.einsum('gnt,gns->gts', left_rows, right_rows, precision=lax.Precision...  63.9 us
    ppermute x16, starting transfers between devices, shifted(): lax.ppermute(value, axis, [(source, source + steps) for source in range(l...  32.3 us
    mul x30, local copies, waits for them, and re-layouts, pass_on(): span_decay[:, :, None] * incoming.reshape(POLES, filter_count, CPG)  32.3 us
    convert_element_type x1, other arithmetic, per_device(): featured = featured.astype(jnp.bfloat16)  28.3 us
    unnamed x45, local copies, waits for them, and re-layouts  14.6 us
    concatenate x1, other arithmetic, per_device(): extended = jnp.concatenate([tail_block, streams], axis=1)  9.47 us
  transfers between devices with their start and end apart: 16, of which 15 were waited for; matrix products, arithmetic and copies ran while one was open for 3% of the time, Pallas kernels for 0%

commit v1 on v0

v1 whole, which is shorter than its diff:
```python
import functools

import jax
import jax.numpy as jnp
from jax import lax
from jax.experimental import pallas as pl
from jax.experimental.pallas import tpu as pltpu
from jax.sharding import PartitionSpec as P

CPG = 16
POLES = 16
TAPS = 7
LANES = 128
UNIT = 16
F32 = jnp.float32
BF16 = jnp.bfloat16


def roll(value, steps):
    return pltpu.roll(value, steps, 0)


def conv_rows(x, taps, before, row, masks=None):
    b1, b2, b_low, b_mid = before
    r1, r2 = roll(x, 1), roll(x, 2)
    low = taps[6] * x
    r_low = roll(low, 3)
    a1 = jnp.where(row < 1, b1, r1)
    a2 = jnp.where(row < 2, b2, r2)
    s_low = jnp.where(row < 3, b_low, r_low)
    if masks is not None:
        a1 = jnp.where(masks[0], a1, 0.0)
        a2 = jnp.where(masks[1], a2, 0.0)
        s_low = jnp.where(masks[2], s_low, 0.0)
    mid = taps[3] * x + taps[4] * a1 + (taps[5] * a2 + s_low)
    r_mid = roll(mid, 3)
    s_mid = jnp.where(row < 3, b_mid, r_mid)
    if masks is not None:
        s_mid = jnp.where(masks[2], s_mid, 0.0)
    out = taps[0] * x + taps[1] * a1 + (taps[2] * a2 + s_mid)
    return out, (r1, r2, r_low, r_mid)


def no_rows():
    zero = jnp.zeros((8, LANES), F32)
    return (zero, zero, zero, zero)


def rounded(value):
    return value.astype(BF16).astype(F32)


def features_kernel(
    starts, q_ref, k_ref, v_ref, halo_ref, taps_ref, lam_ref, res_ref,
    query_ref, local_ref, span_ref, xs, ys, *, rows, genomes,
):
    tiles = q_ref.shape[1] // LANES
    row = lax.broadcasted_iota(jnp.int32, (8, LANES), 0)
    streams = (q_ref, k_ref, v_ref)

    def tap_rows(stream, lanes):
        return [
            jnp.broadcast_to(taps_ref[stream, j : j + 1, lanes], (8, LANES)) for j in range(TAPS)
        ]

    def emit(tile, lanes, unit_row, q_pair, k_pair, v_pair):
        query_ref[pl.ds(unit_row, UNIT), lanes] = jnp.concatenate(q_pair, 0).astype(BF16)
        mixed = jnp.concatenate(
            [rounded(k) * rounded(v) for k, v in zip(k_pair, v_pair)], 0
        )
        xs[pl.ds(pl.multiple_of(tile * rows + unit_row, UNIT), UNIT), :] = mixed

    def tile_body(tile, _):
        lanes = pl.ds(pl.multiple_of(tile * LANES, LANES), LANES)
        taps = [tap_rows(s, lanes) for s in range(3)]
        carry = []
        for s in range(3):
            halo = halo_ref[s, :, lanes].astype(F32)
            carry.append(conv_rows(halo, taps[s], no_rows(), row)[1])
        for unit in range(rows // UNIT):
            pairs = []
            for s in range(3):
                x16 = streams[s][unit * UNIT : (unit + 1) * UNIT, lanes].astype(F32)
                y0, c = conv_rows(x16[:8], taps[s], carry[s], row)
                y1, c = conv_rows(x16[8:], taps[s], c, row)
                carry[s] = c
                pairs.append((y0, y1))
            emit(tile, lanes, unit * UNIT, *pairs)
        return 0

    lax.fori_loop(0, tiles, tile_body, 0)

    def patch(unit):
        unit_row = pl.multiple_of(unit * UNIT, UNIT)
        above = pl.multiple_of(jnp.maximum(unit - 1, 0) * UNIT, UNIT)

        def masks_at(first):
            at = first + row
            out = []
            for reach in (1, 2, 3):
                bad = jnp.zeros((8, LANES), jnp.bool_)
                for g in range(genomes):
                    bad = bad | ((at >= starts[g]) & (at < starts[g] + reach))
                out.append(jnp.logical_not(bad))
            return out

        masks = [masks_at(unit_row - 8), masks_at(unit_row), masks_at(unit_row + 8)]

        def patch_tile(tile, _):
            lanes = pl.ds(pl.multiple_of(tile * LANES, LANES), LANES)
            pairs = []
            for s in range(3):
                taps = tap_rows(s, lanes)
                halo = halo_ref[s, :, lanes].astype(F32)
                prev = streams[s][pl.ds(above, UNIT), lanes].astype(F32)[8:]
                prev = jnp.where(unit == 0, halo, prev)
                x16 = streams[s][pl.ds(unit_row, UNIT), lanes].astype(F32)
                c = conv_rows(prev, taps, no_rows(), row, masks[0])[1]
                y0, c = conv_rows(x16[:8], taps, c, row, masks[1])
                y1, c = conv_rows(x16[8:], taps, c, row, masks[2])
                pairs.append((y0, y1))
            emit(tile, lanes, unit_row, *pairs)
            return 0

        lax.fori_loop(0, tiles, patch_tile, 0)

    for g in range(genomes):
        start = starts[g]
        first = jnp.maximum(start, 0) // UNIT
        last = jnp.minimum(start + TAPS - 2, rows - 1) // UNIT
        near = (start > 1 - TAPS) & (start < rows)

        @pl.when(near)
        def _():
            patch(first)

        @pl.when(near & (last != first))
        def _():
            patch(last)

    decay = [jnp.exp(-lam_ref[n]) for n in range(POLES)]
    weight = [res_ref[n] for n in range(POLES)]

    def steps(first, state, keeps):
        state = list(state)
        for r in range(8):
            x = xs[pl.ds(first + r, tiles, stride=rows), :]
            parts = []
            for n in range(POLES):
                old = state[n] if keeps is None else state[n] * keeps[r]
                state[n] = decay[n] * old + x
                parts.append(weight[n] * state[n])
            while len(parts) > 1:
                parts = [a + b for a, b in zip(parts[::2], parts[1::2])]
            ys[pl.ds(first + r, tiles, stride=rows), :] = parts[0]
        return tuple(state)

    def eight(i, state):
        first = pl.multiple_of(i * 8, 8)
        cut = functools.reduce(
            jnp.logical_or,
            [(starts[g] >= first) & (starts[g] < first + 8) for g in range(genomes)],
        )

        def broken(state):
            keeps = []
            for r in range(8):
                here = functools.reduce(
                    jnp.logical_or, [starts[g] == first + r for g in range(genomes)]
                )
                keeps.append(jnp.where(here, 0.0, 1.0))
            return steps(first, state, keeps)

        return lax.cond(cut, broken, lambda s: steps(first, s, None), state)

    zero = jnp.zeros((tiles, LANES), F32)
    final = lax.fori_loop(0, rows // 8, eight, (zero,) * POLES)
    for n in range(POLES):
        span_ref[n] = final[n]
    for tile in range(tiles):
        local_ref[:, tile * LANES : (tile + 1) * LANES] = ys[tile * rows : (tile + 1) * rows, :]


def gate_kernel(
    starts, core_ref, local_ref, query_ref, mine_ref, other_ref, lam_ref, res_ref, out_ref,
    *, rows, genomes,
):
    group = pl.program_id(0)
    tiles = 2 * LANES // LANES
    half = pl.num_programs(0) // 2
    use_mine = (group // half) == core_ref[0]
    first = (group % half) * tiles
    pieces = []
    for t in range(tiles):
        at = pl.ds(first + t, POLES, stride=half * tiles)
        pieces.append(jnp.where(use_mine, mine_ref[at, :], other_ref[at, :]))
    state = jnp.concatenate(pieces, 1)
    width = state.shape[1]
    filters = width // CPG
    lane_filter = lax.broadcasted_iota(jnp.int32, (POLES, width), 1) // CPG
    hi = state.astype(BF16)
    lo = (state - hi.astype(F32)).astype(BF16)

    def spread(value):
        wide = value.astype(F32)
        return jnp.concatenate(
            [jnp.where(lane_filter == f, wide, 0.0).astype(BF16) for f in range(filters)], 0
        )

    s_hi, s_lo = spread(hi), spread(lo)
    t = lax.broadcasted_iota(jnp.int32, (rows, width), 0)
    keep = jnp.ones((rows, width), jnp.bool_)
    for g in range(genomes):
        keep = keep & jnp.logical_not((starts[g] >= 0) & (t >= starts[g]))
    power = res_ref[0] * jnp.exp(-lam_ref[0] * (t + 1).astype(F32))
    power = jnp.where(keep, power, 0.0)
    e_hi = power.astype(BF16)
    e_lo = (power - e_hi.astype(F32)).astype(BF16)
    dot = functools.partial(jnp.dot, preferred_element_type=F32)
    filtered = local_ref[...] + dot(e_hi, s_hi) + (dot(e_lo, s_hi) + dot(e_hi, s_lo))
    out_ref[...] = (query_ref[...].astype(F32) * filtered).astype(BF16)


def exchange(value, pairs):
    return lax.ppermute(value, "ctx", pairs)


def per_device(q_in, k_in, v_in, conv_filter, decay_rate, residue, genome_lengths):
    rows, width = q_in.shape
    filters = width // CPG
    tiles = width // LANES
    genomes = genome_lengths.shape[0]
    count = lax.axis_size("ctx")
    index = lax.axis_index("ctx")
    starts = jnp.cumsum(genome_lengths) - genome_lengths
    relative = (starts - index * rows).astype(jnp.int32)

    tail = jnp.stack([q_in[rows - 8 :], k_in[rows - 8 :], v_in[rows - 8 :]])
    halo = exchange(tail, [(i, i + 1) for i in range(count - 1)])

    lam_wide = jnp.repeat(decay_rate.T, CPG, axis=1).reshape(POLES, tiles, LANES)
    res_wide = jnp.repeat(residue.T, CPG, axis=1).reshape(POLES, tiles, LANES)

    block = 8 * LANES
    stream_spec = pl.BlockSpec((rows, block), lambda b, *_: (0, b))
    wide_spec = pl.BlockSpec((POLES, 8, LANES), lambda b, *_: (0, b, 0))
    query, local, span = pl.pallas_call(
        functools.partial(features_kernel, rows=rows, genomes=genomes),
        grid_spec=pltpu.PrefetchScalarGridSpec(
            num_scalar_prefetch=1,
            grid=(width // block,),
            in_specs=[
                stream_spec, stream_spec, stream_spec,
                pl.BlockSpec((3, 8, block), lambda b, *_: (0, 0, b)),
                pl.BlockSpec((3, TAPS, block), lambda b, *_: (0, 0, b)),
                wide_spec, wide_spec,
            ],
            out_specs=[stream_spec, stream_spec, wide_spec],
            scratch_shapes=[
                pltpu.VMEM((8 * rows, LANES), F32),
                pltpu.VMEM((8 * rows, LANES), F32),
            ],
        ),
        out_shape=[
            jax.ShapeDtypeStruct((rows, width), BF16),
            jax.ShapeDtypeStruct((rows, width), F32),
            jax.ShapeDtypeStruct((POLES, tiles, LANES), F32),
        ],
        name="features",
    )(relative, q_in, k_in, v_in, halo, conv_filter, lam_wide, res_wide)

    def end_id(device):
        return jnp.sum((starts <= (device + 1) * rows - 1).astype(jnp.int32))

    def joined(a, b):
        return (end_id(a) == end_id(b)).astype(F32)

    core = index % 2
    half = tiles // 2
    lam_mine = lax.dynamic_slice_in_dim(lam_wide, core * half, half, 1)

    def power(devices):
        return jnp.exp(-lam_mine * (rows * devices).astype(F32))

    one = jnp.int32(1)
    away = [(i, i ^ 1) for i in range(count)]
    given = lax.dynamic_slice_in_dim(span, (1 - core) * half, half, 1)
    own = lax.dynamic_slice_in_dim(span, core * half, half, 1)
    got = exchange(given, away)
    left = jnp.where(core == 0, own, got)
    right = jnp.where(core == 0, got, own)
    chip_first = index - core
    total = power(one) * joined(chip_first, chip_first + 1) * left + right
    prefix = jnp.zeros_like(total)
    size = 2
    while size < count:
        other = exchange(total, [(i, i ^ size) for i in range(count)])
        is_right = (index // size) % 2 == 1
        block_first = index // size * size
        block_last = block_first + size - 1
        before = block_first - 1
        into = power(chip_first - block_first) * joined(before, chip_first - 1) * other
        prefix = prefix + jnp.where(is_right, into, 0.0)
        gain = power(jnp.int32(size))
        as_right = gain * joined(before, block_last) * other + total
        as_left = gain * joined(block_last, block_last + size) * total + other
        total = jnp.where(is_right, as_right, as_left)
        size *= 2
    second = power(one) * joined(chip_first - 1, chip_first) * prefix + left
    mine = jnp.where(core == 0, prefix, second)
    others = jnp.where(core == 0, second, prefix)
    back = exchange(others, away)

    groups = filters // 16
    lane_spec = pl.BlockSpec((rows, 2 * LANES), lambda b, *_: (0, b))
    flat_spec = pl.BlockSpec((1, 1, 2 * LANES), lambda b, *_: (b, 0, 0))
    whole = pl.BlockSpec((POLES * half, LANES), lambda b, *_: (0, 0))
    return pl.pallas_call(
        functools.partial(gate_kernel, rows=rows, genomes=genomes),
        grid_spec=pltpu.PrefetchScalarGridSpec(
            num_scalar_prefetch=2,
            grid=(groups,),
            in_specs=[lane_spec, lane_spec, whole, whole, flat_spec, flat_spec],
            out_specs=lane_spec,
        ),
        out_shape=jax.ShapeDtypeStruct((rows, width), BF16),
        name="gate",
    )(
        relative, jnp.reshape(core, (1,)).astype(jnp.int32), local, query,
        mine.reshape(POLES * half, LANES), back.reshape(POLES * half, LANES),
        decay_rate.reshape(groups, 1, 2 * LANES), residue.reshape(groups, 1, 2 * LANES),
    )


def solution(mesh):
    in_specs = (
        P(("groups", "ctx"), None),
        P(("groups", "ctx"), None),
        P(("groups", "ctx"), None),
        P(),
        P(),
        P(),
        P("groups"),
    )
    return jax.shard_map(
        per_device, mesh=mesh, in_specs=in_specs, out_specs=P(("groups", "ctx"), None), check_vma=False
    )
```

time: 409 us -> 85.6 us (0.21)
  the two profiles are of different devices: /device:TPU:18 before, /device:TPU:0 now
where the time goes in v1:
time: 85.6 us; the launch traced here: 85.5 us
  Pallas kernels  48.4 us (57%)
  between operations  11.9 us (14%)
  local copies, waits for them, and re-layouts  10.1 us (12%)
  waiting for transfers between devices  6.27 us (7%)
  starting transfers between devices  4.75 us (6%)
  other arithmetic  4.13 us (5%)
    pallas_call x1, Pallas kernels, per_device(): pl.pallas_call(functools.partial(features_kernel, rows=rows, genomes=geno...  34.1 us
    pallas_call x1, Pallas kernels, per_device(): pl.pallas_call(functools.partial(gate_kernel, rows=rows, genomes=genomes)...  14.3 us
    ppermute x6, waiting for transfers between devices, exchange(): return lax.ppermute(value, 'ctx', pairs)  6.27 us
    ppermute x6, starting transfers between devices, exchange(): return lax.ppermute(value, 'ctx', pairs)  4.75 us
    another operation x2, local copies, waits for them, and re-layouts, per_device(): tail = jnp.stack([q_in[rows - 8:], k_in[rows - 8:], v_in[rows - 8:]])  1.72 us
  transfers between devices with their start and end apart: 6, of which 3 were waited for; matrix products, arithmetic and copies ran while one was open for 10% of the time, Pallas kernels for 0%

profile of v1, /device:TPU:0, one launch (start us, length us, event | category | flops | bytes accessed | tf_op | source)
XLA Modules:
  0.0 85.5 jit_solution(6991080644113572296)
XLA Ops:
  0.0 0.8 slice_bitcast_fusion.2
  0.8 0.9 %slice_bitcast_fusion = (bf16[1,8,4096]{2,1,0:T(8,128)(2,1)S(1)}, bf16[1,8,4096]{2,1,0:T(8,128)(2,1)S(1)}) fusion(bf16[256,4096]{1,0:T(8,128)(2,1)} %v_ref.1, bf16[256,4096]{1,0:T(8,128)(2,1)} %k_ref.1), kind=kLoop, calls=%fused_computation.9 | loop fusion | bytes 262144 | tf_op jit(solution)/shard_map/stack | solution.py:238
  1.8 2.4 %collective-permute-start = (bf16[3,8,4096]{2,1,0:T(8,128)(2,1)S(1)}, bf16[3,8,4096]{2,1,0:T(8,128)(2,1)S(1)}, u32[]{:S(2)}, u32[]{:S(2)}) collective-permute-start(bf16[3,8,4096]{2,1,0:T(8,128)(2,1)S(1)} %pad_maximum_fusion), channel_id=1, source_target_pairs={{0,1},{1,2},{2,3},{3,4},{4,5},{5,6},{6,7},{7,8},{8,9},{9,10},{10,1... | collective-permute-start | bytes 589832 | tf_op jit(solution)/shard_map/ppermute | solution.py:225
  4.2 0.8 reduce-window.9
  5.1 1.3 %broadcast_in_dim.13 = f32[16,256,16]{2,1,0:T(8,128)S(1)} broadcast(f32[16,256]{1,0:T(8,128)} %bitcast.18), dimensions={0,1} | broadcast | bytes 278528 | tf_op jit(solution)/shard_map/broadcast_in_dim | solution.py:242
  6.4 1.3 %reshape_reshape.7.res_ref = f32[16,32,128]{2,1,0:T(8,128)} reshape(f32[16,256,16]{2,1,0:T(8,128)S(1)} %broadcast_in_dim.13) | data formatting | bytes 524288 | tf_op jit(solution)/shard_map/reshape;reshape | solution.py:242
  7.7 0.6 broadcast_in_dim.12
  8.3 1.3 %reshape_reshape.6.lam_ref = f32[16,32,128]{2,1,0:T(8,128)} reshape(f32[16,256,16]{2,1,0:T(8,128)S(1)} %broadcast_in_dim.12) | data formatting | bytes 524288 | tf_op jit(solution)/shard_map/reshape;reshape | solution.py:241
  9.5 0.8 fusion.1
  10.4 0.5 broadcast_subtract_fusion.starts
  10.9 0.7 copy-done.2
  11.6 34.1 %features.1 = (bf16[256,4096]{1,0:T(8,128)(2,1)}, f32[256,4096]{1,0:T(8,128)}, f32[16,32,128]{2,1,0:T(8,128)}) custom-call(s32[4]{0:T(128)} %broadcast_subtract_fusion.starts, bf16[256,4096]{1,0:T(8,128)(2,1)} %q_ref.1, bf16[256,4096]{1,0:T(8,128)(2,1)} %k_ref.1, bf16[256,4096]{1,0:T(8,128)(2,1)} %v_ref.1, bf16[3,8,4096]{2,1,0:T(8,128)(2,1)} %copy-done.2, ...), custom_call_target="tpu_custom_call" | custom-call | tf_op jit(solution)/shard_map/features/pallas_call | solution.py:247
  45.7 1.0 %constant_dynamic-slice_fusion = f32[16,16,128]{2,1,0:T(8,128)S(1)} fusion(f32[16,32,128]{2,1,0:T(8,128)} %get-tuple-element.10, s32[]{:T(128)S(6)} %select_n.93), kind=kLoop, calls=%fused_computation.24 | loop fusion | bytes 262148 | tf_op jit(solution)/shard_map/dynamic_slice | solution.py:287
  46.7 0.1 collective-permute-start.1
  48.1 1.0 %select_add_fusion.1 = f32[16,16,128]{2,1,0:T(8,128)S(1)} fusion(f32[16,16,128]{2,1,0:T(8,128)S(1)} %collective-permute-done.1, f32[16,32,128]{2,1,0:T(8,128)} %get-tuple-element.10, s32[]{:T(128)S(6)} %select_n.92, f32[16,32,128]{2,1,0:T(8,128)S(1)} %copy-done, f32[]{:T(128)S(6)} %convert_element_type.80, pred[]{:T(512)S(6)} %eq.47), kind=kLoop, calls=%fused_computation.5 | loop fusion | flops 229376 | bytes 524297 | tf_op jit(solution)/shard_map/add | solution.py:293
  49.1 0.1 collective-permute-start.2
  51.8 3.2 %collective-permute-done.2 = f32[16,16,128]{2,1,0:T(8,128)S(1)} collective-permute-done((f32[16,16,128]{2,1,0:T(8,128)S(1)}, f32[16,16,128]{2,1,0:T(8,128)S(1)}, u32[]{:S(2)}, u32[]{:S(2)}) %collective-permute-start.2) | collective-permute-done | bytes 131104 | tf_op jit(solution)/shard_map/ppermute | solution.py:225
  55.0 0.1 add_select_fusion.1
  55.1 0.1 collective-permute-start.3
  57.8 2.4 %collective-permute-done.3 = f32[16,16,128]{2,1,0:T(8,128)S(1)} collective-permute-done((f32[16,16,128]{2,1,0:T(8,128)S(1)}, f32[16,16,128]{2,1,0:T(8,128)S(1)}, u32[]{:S(2)}, u32[]{:S(2)}) %collective-permute-start.3) | collective-permute-done | bytes 131104 | tf_op jit(solution)/shard_map/ppermute | solution.py:225
  60.2 0.1 add_select_fusion
  60.3 2.1 %collective-permute-start.4 = (f32[16,16,128]{2,1,0:T(8,128)S(1)}, f32[16,16,128]{2,1,0:T(8,128)S(1)}, u32[]{:S(2)}, u32[]{:S(2)}) collective-permute-start(f32[16,16,128]{2,1,0:T(8,128)S(1)} %add_select_fusion), channel_id=1, source_target_pairs={{0,8},{1,9},{2,10},{3,11},{4,12},{5,13},{6,14},{7,15},{8,0},{9,1},... | collective-permute-start | bytes 393224 | tf_op jit(solution)/shard_map/ppermute | solution.py:225
  66.2 0.1 copy.10
  66.3 0.1 copy.11
  67.7 0.7 reshape.48.lam_ref
  68.4 0.7 reshape.49.res_ref
  69.1 0.1 broadcast_select_fusion
  69.2 0.1 collective-permute-start.5
  69.3 0.7 broadcast_select_fusion.1
  70.0 0.6 collective-permute-done.5
  70.6 0.6 copy-done.3
  71.3 14.3 %gate.1 = bf16[256,4096]{1,0:T(8,128)(2,1)} custom-call(s32[4]{0:T(128)} %broadcast_subtract_fusion.starts, s32[1]{0:T(128)} %bitcast.2.core_ref, f32[256,4096]{1,0:T(8,128)} %get-tuple-element.8.local_ref, bf16[256,4096]{1,0:T(8,128)(2,1)} %get-tuple-element.9.query_ref, f32[256,128]{1,0:T(8,128)} %bitcast.15, f32[256,128]{1,0:T(8,128)} %bitcast.16, ...), custom_call_target="tpu_custom_call" | custom-call | tf_op jit(solution)/shard_map/gate/pallas_call | solution.py:318
  (16 shorter events, 0.1 us)
Async XLA Ops:
  1.8 9.2 %collective-permute-start = (bf16[3,8,4096]{2,1,0:T(8,128)(2,1)S(1)}, bf16[3,8,4096]{2,1,0:T(8,128)(2,1)S(1)}, u32[]{:S(2)}, u32[]{:S(2)}) collective-permute-start(bf16[3,8,4096]{2,1,0:T(8,128)(2,1)S(1)} %pad_maximum_fusion), channel_id=1, source_target_pairs={{0,1},{1,2},{2,3},{3,4},{4,5},{5,6},{6,7},{7,8},{8,9},{9,10},{10,1... | collective-permute-start | bytes 589832 | tf_op jit(solution)/shard_map/ppermute | solution.py:225
  5.1 2.6 %copy-start.4 = (f32[256,16]{0,1:T(8,128)S(1)}, f32[256,16]{0,1:T(8,128)}, u32[]{:S(2)}) copy-start(f32[256,16]{0,1:T(8,128)} %param.11) | copy-start | bytes 49156
  7.7 1.9 %copy-start.6 = (s32[4]{0:T(128)S(1)}, s32[4]{0:T(128)}, u32[]{:S(2)}) copy-start(s32[4]{0:T(128)} %param.13) | copy-start | bytes 52
  10.9 37.2 %copy-start = (f32[16,32,128]{2,1,0:T(8,128)S(1)}, f32[16,32,128]{2,1,0:T(8,128)}, u32[]{:S(2)}) copy-start(f32[16,32,128]{2,1,0:T(8,128)} %reshape_reshape.6.lam_ref) | copy-start | bytes 786436
  10.9 0.7 copy-start.2
  45.7 20.6 %copy-start.5 = (f32[256,16]{0,1:T(8,128)S(1)}, f32[256,16]{0,1:T(8,128)}, u32[]{:S(2)}) copy-start(f32[256,16]{0,1:T(8,128)} %param.12) | copy-start | bytes 49156
  45.7 23.4 %copy-start.1 = (f32[16,32,128]{2,1,0:T(8,128)S(1)}, f32[16,32,128]{2,1,0:T(8,128)}, u32[]{:S(2)}) copy-start(f32[16,32,128]{2,1,0:T(8,128)} %get-tuple-element.10) | copy-start | bytes 786436
  46.7 1.4 %collective-permute-start.1 = (f32[16,16,128]{2,1,0:T(8,128)S(1)}, f32[16,16,128]{2,1,0:T(8,128)S(1)}, u32[]{:S(2)}, u32[]{:S(2)}) collective-permute-start(f32[16,16,128]{2,1,0:T(8,128)S(1)} %constant_dynamic-slice_fusion), channel_id=1, source_target_pairs={{0,1},{1,0},{2,3},{3,2},{4,5},{5,4},{6,7},{7,6},{8,9},{9,8},{10,11... | collective-permute-start | bytes 393224 | tf_op jit(solution)/shard_map/ppermute | solution.py:225
  49.1 6.0 %collective-permute-start.2 = (f32[16,16,128]{2,1,0:T(8,128)S(1)}, f32[16,16,128]{2,1,0:T(8,128)S(1)}, u32[]{:S(2)}, u32[]{:S(2)}) collective-permute-start(f32[16,16,128]{2,1,0:T(8,128)S(1)} %select_add_fusion.1), channel_id=1, source_target_pairs={{0,2},{1,3},{2,0},{3,1},{4,6},{5,7},{6,4},{7,5},{8,10},{9,11},{10,... | collective-permute-start | bytes 393224 | tf_op jit(solution)/shard_map/ppermute | solution.py:225
  55.1 5.1 %collective-permute-start.3 = (f32[16,16,128]{2,1,0:T(8,128)S(1)}, f32[16,16,128]{2,1,0:T(8,128)S(1)}, u32[]{:S(2)}, u32[]{:S(2)}) collective-permute-start(f32[16,16,128]{2,1,0:T(8,128)S(1)} %add_select_fusion.1), channel_id=1, source_target_pairs={{0,4},{1,5},{2,6},{3,7},{4,0},{5,1},{6,2},{7,3},{8,12},{9,13},{10,... | collective-permute-start | bytes 393224 | tf_op jit(solution)/shard_map/ppermute | solution.py:225
  60.3 8.8 %collective-permute-start.4 = (f32[16,16,128]{2,1,0:T(8,128)S(1)}, f32[16,16,128]{2,1,0:T(8,128)S(1)}, u32[]{:S(2)}, u32[]{:S(2)}) collective-permute-start(f32[16,16,128]{2,1,0:T(8,128)S(1)} %add_select_fusion), channel_id=1, source_target_pairs={{0,8},{1,9},{2,10},{3,11},{4,12},{5,13},{6,14},{7,15},{8,0},{9,1},... | collective-permute-start | bytes 393224 | tf_op jit(solution)/shard_map/ppermute | solution.py:225
  69.2 1.4 %collective-permute-start.5 = (f32[16,16,128]{2,1,0:T(8,128)S(1)}, f32[16,16,128]{2,1,0:T(8,128)S(1)}, u32[]{:S(2)}, u32[]{:S(2)}) collective-permute-start(f32[16,16,128]{2,1,0:T(8,128)S(1)} %get-tuple-element.21), channel_id=1, source_target_pairs={{0,1},{1,0},{2,3},{3,2},{4,5},{5,4},{6,7},{7,6},{8,9},{9,8},{10,11... | collective-permute-start | bytes 393224 | tf_op jit(solution)/shard_map/ppermute | solution.py:225
  70.6 0.7 copy-start.3

commit v2 on v0

v2 whole, which is shorter than its diff:
```python
import functools

import jax
import jax.numpy as jnp
from jax import lax
from jax.experimental import pallas as pl
from jax.experimental.pallas import tpu as pltpu
from jax.sharding import PartitionSpec as P

CPG = 16
POLES = 16
TAPS = 7
LANES = 128
UNIT = 16
GROUP = LANES // CPG
F32 = jnp.float32
BF16 = jnp.bfloat16


def iota(shape, axis):
    return lax.broadcasted_iota(jnp.int32, shape, axis)


def lanes_of(tile):
    if isinstance(tile, int):
        return slice(tile * LANES, (tile + 1) * LANES)
    return pl.ds(pl.multiple_of(tile * LANES, LANES), LANES)


def split(value):
    hi = value.astype(BF16)
    return hi, (value - hi.astype(F32)).astype(BF16)


def any_of(flags):
    return functools.reduce(jnp.logical_or, flags)


def conv_terms(taps, window):
    terms = [taps[j] * window(j) for j in range(TAPS)]
    even = (terms[0] + terms[1]) + (terms[2] + terms[3])
    return even + ((terms[4] + terms[5]) + terms[6])


def short_conv(starts, streams, halo_refs, taps_refs, xs, emit, tiles, rows, genomes):
    count = len(streams)
    cut_above = functools.reduce(
        jnp.maximum, [jnp.where(starts[g] <= 0, starts[g], -rows) for g in range(genomes)]
    )
    halo_kept = iota((8, LANES), 0) - 8 >= cut_above

    def base(tile, _):
        lanes = lanes_of(tile)
        for s in range(count):
            xs[s, tile, :8] = jnp.where(halo_kept, halo_refs[s][:, lanes].astype(F32), 0.0)
            xs[s, tile, 8:] = streams[s][:, lanes].astype(F32)
        taps = [
            [jnp.broadcast_to(taps_refs[s][j : j + 1, lanes], (8, LANES)) for j in range(TAPS)]
            for s in range(count)
        ]
        for r in range(0, rows, UNIT):
            done = []
            for s in range(count):
                for at in (r + 8, r + 16):
                    done.append(
                        conv_terms(
                            taps[s], lambda j, s=s, at=at: xs[s, tile, at - j : at - j + 8]
                        )
                    )
            emit(tile, lanes, r, done)
        return 0

    lax.fori_loop(0, tiles, base, 0)

    def patch(unit):
        first = pl.multiple_of(unit * UNIT, UNIT)
        cuts = []
        for h in range(2):
            at = first + 8 * h + iota((8, LANES), 0)
            cuts.append(
                [
                    any_of([(at >= starts[g]) & (at < starts[g] + j) for g in range(genomes)])
                    for j in range(1, TAPS)
                ]
            )

        def patch_tile(tile, _):
            lanes = lanes_of(tile)
            done = []
            for s in range(count):
                taps = [taps_refs[s][j : j + 1, lanes] for j in range(TAPS)]
                for h in range(2):

                    def window(j, s=s, h=h):
                        moved = xs[s, tile, pl.ds(first + 8 * (h + 1) - j, 8)]
                        return moved if j == 0 else jnp.where(cuts[h][j - 1], 0.0, moved)

                    done.append(conv_terms(taps, window))
            emit(tile, lanes, first, done)
            return 0

        lax.fori_loop(0, tiles, patch_tile, 0)

    for g in range(genomes):
        start = starts[g]
        inside = (start > 0) & (start < rows)
        unit = start // UNIT
        end = jnp.minimum(start + TAPS - 2, rows - 1) // UNIT

        @pl.when(inside)
        def _():
            patch(unit)

        @pl.when(inside & (end != unit))
        def _():
            patch(end)


def expand_kernel(lam_ref, res_ref, lam_rows, res_rows, lam_wide, *, tiles):
    parts = []
    for source in (lam_ref, res_ref):
        rest = source[...]
        for _ in range(3):
            part = rest.astype(BF16)
            rest = rest - part.astype(F32)
            parts.append(part)
    parts = jnp.concatenate(parts, 0)
    for pair in range(tiles // 2):
        first = pair * 2 * GROUP
        side = first // LANES * LANES
        shape = (LANES, 2 * LANES)
        pick = iota(shape, 1) // CPG + (first - side) == iota(shape, 0)
        wide = jnp.dot(
            parts[:, side : side + LANES], jnp.where(pick, 1.0, 0.0).astype(BF16),
            preferred_element_type=F32,
        )
        wide = [wide[i * POLES : (i + 1) * POLES] for i in range(6)]
        lam = wide[0] + wide[1] + wide[2]
        res = wide[3] + wide[4] + wide[5]
        lam_wide[:, 2 * pair * LANES : (2 * pair + 2) * LANES] = lam
        for t in range(2):
            lam_rows[:, 2 * pair + t, :] = lam[:, lanes_of(t)]
            res_rows[:, 2 * pair + t, :] = res[:, lanes_of(t)]


def states_kernel(
    starts, k_ref, v_ref, k_halo, v_halo, taps_ref, lam_ref, res_ref,
    local_ref, span_ref, xs, mixed, final, *, rows, genomes,
):
    tiles = k_ref.shape[1] // LANES

    def emit(tile, lanes, first, done):
        k0, k1, v0, v1 = (value.astype(BF16).astype(F32) for value in done)
        row = pl.ds(pl.multiple_of(tile * 8, 8), 8)
        mixed[first // 8, row, :] = k0 * v0
        mixed[first // 8 + 1, row, :] = k1 * v1

    short_conv(
        starts, (k_ref, v_ref), (k_halo.at[0], v_halo.at[0]), (taps_ref.at[1], taps_ref.at[2]),
        xs, emit, tiles, rows, genomes,
    )
    decay = [jnp.exp(-lam_ref[n]) for n in range(POLES)]
    weight = [res_ref[n] for n in range(POLES)]

    def one(eight, r, state, keep=None):
        x = mixed[eight, pl.ds(r, tiles, stride=8), :]
        out, sums = [], [None, None]
        for n in range(POLES):
            old = state[n] if keep is None else state[n] * keep
            new = decay[n] * old + x
            term = weight[n] * new
            sums[n % 2] = term if sums[n % 2] is None else sums[n % 2] + term
            out.append(new)
        local_ref[eight, pl.ds(r, tiles, stride=8), :] = sums[0] + sums[1]
        return out

    size = 32

    def block(i, state):
        first = i * size
        cut = any_of(
            [(starts[g] > 0) & (starts[g] >= first) & (starts[g] < first + size) for g in range(genomes)]
        )

        def smooth(state):
            state = list(state)
            for r in range(size):
                state = one(i * (size // 8) + r // 8, r % 8, state)
            return tuple(state)

        def broken(state):
            def step(t, state):
                here = any_of([starts[g] == first + t for g in range(genomes)])
                keep = jnp.where(here, 0.0, 1.0)
                return tuple(one(i * (size // 8) + t // 8, t % 8, list(state), keep))

            return lax.fori_loop(0, size, step, state, unroll=8)

        return lax.cond(cut, broken, smooth, state)

    zero = jnp.zeros((tiles, LANES), F32)
    state = lax.fori_loop(0, rows // size, block, (zero,) * POLES)
    for n in range(POLES):
        final[n * tiles : (n + 1) * tiles, :] = state[n]
    for tile in range(tiles):
        span_ref[:, lanes_of(tile)] = final[pl.ds(tile, POLES, stride=tiles), :]


def query_kernel(starts, q_ref, q_halo, taps_ref, query_ref, xs, *, rows, genomes):
    def emit(tile, lanes, first, done):
        query_ref[pl.ds(first, UNIT), lanes] = jnp.concatenate(done, 0).astype(BF16)

    short_conv(
        starts, (q_ref,), (q_halo.at[0],), (taps_ref.at[0],), xs, emit,
        q_ref.shape[1] // LANES, rows, genomes,
    )


def gate_kernel(
    starts, core_ref, local_ref, query_ref, mine_ref, other_ref, lam_ref, res_ref, out_ref,
    *, rows, genomes,
):
    width = 2 * LANES
    filters = width // CPG
    use_mine = (pl.program_id(0) // (pl.num_programs(0) // 2)) == core_ref[0]
    lane_filter = iota((POLES, width), 1) // CPG
    t = iota((rows, width), 0)
    keep = jnp.logical_not(any_of([(starts[g] >= 0) & (t >= starts[g]) for g in range(genomes)]))
    ahead = jnp.where(keep, (t + 1).astype(F32), 1e9)
    dot = functools.partial(jnp.dot, preferred_element_type=F32)

    def spread(value):
        zero = jnp.zeros((), BF16)
        return jnp.concatenate(
            [jnp.where(lane_filter == f, value, zero) for f in range(filters)], 0
        )

    for group in range(out_ref.shape[1] // width):
        lanes = slice(group * width, (group + 1) * width)
        state = jnp.where(use_mine, mine_ref[:, lanes], other_ref[:, lanes])
        hi, lo = split(state)
        s_hi, s_lo = spread(hi), spread(lo)
        e_hi, e_lo = split(res_ref[group] * jnp.exp(-lam_ref[group] * ahead))
        carried = dot(e_hi, s_hi) + (dot(e_lo, s_hi) + dot(e_hi, s_lo))
        local = jnp.concatenate(
            [
                local_ref[:, (2 * group + t) * 8 : (2 * group + t + 1) * 8, :].reshape(rows, LANES)
                for t in range(2)
            ],
            1,
        )
        filtered = local + carried
        out_ref[:, lanes] = (query_ref[:, lanes].astype(F32) * filtered).astype(BF16)


def exchange(value, pairs):
    return lax.ppermute(value, "ctx", pairs)


def per_device(q_in, k_in, v_in, conv_filter, decay_rate, residue, genome_lengths):
    rows, width = q_in.shape
    tiles = width // LANES
    genomes = genome_lengths.shape[0]
    count = lax.axis_size("ctx")
    index = lax.axis_index("ctx")
    order = jnp.arange(genomes)
    starts = jnp.sum(jnp.where(order[None, :] < order[:, None], genome_lengths[None, :], 0), 1)
    relative = (starts - index * rows).astype(jnp.int32)

    tail = jnp.stack([x[rows - 8 :] for x in (q_in, k_in, v_in)])
    halo = exchange(tail, [(i, i + 1) for i in range(count - 1)])

    block = 8 * LANES
    steps = width // block
    stream = pl.BlockSpec((rows, block), lambda b, *_: (0, b))
    taps_spec = pl.BlockSpec((3, TAPS, block), lambda b, *_: (0, 0, b))
    row_spec = pl.BlockSpec((POLES, 8, LANES), lambda b, *_: (0, b, 0))
    local_spec = pl.BlockSpec((rows // 8, 8 * 8, LANES), lambda b, *_: (0, b, 0))
    local_shape = jax.ShapeDtypeStruct((rows // 8, tiles * 8, LANES), F32)

    def halo_spec(s):
        return pl.BlockSpec((1, 8, block), lambda b, *_: (s, 0, b))

    lam_rows, res_rows, lam_wide = pl.pallas_call(
        functools.partial(expand_kernel, tiles=tiles),
        out_shape=[
            jax.ShapeDtypeStruct((POLES, tiles, LANES), F32),
            jax.ShapeDtypeStruct((POLES, tiles, LANES), F32),
            jax.ShapeDtypeStruct((POLES, width), F32),
        ],
        name="expand",
        cost_estimate=pl.CostEstimate(flops=10**9, bytes_accessed=10**6, transcendentals=0),
    )(decay_rate.T, residue.T)

    local, span = pl.pallas_call(
        functools.partial(states_kernel, rows=rows, genomes=genomes),
        grid_spec=pltpu.PrefetchScalarGridSpec(
            num_scalar_prefetch=1,
            grid=(steps,),
            in_specs=[
                stream, stream, halo_spec(1), halo_spec(2), taps_spec, row_spec, row_spec
            ],
            out_specs=[local_spec, pl.BlockSpec((POLES, block), lambda b, *_: (0, b))],
            scratch_shapes=[
                pltpu.VMEM((2, 8, rows + 8, LANES), F32),
                pltpu.VMEM((rows // 8, 8 * 8, LANES), F32),
                pltpu.VMEM((POLES * 8, LANES), F32),
            ],
        ),
        out_shape=[local_shape, jax.ShapeDtypeStruct((POLES, width), F32)],
        name="states",
    )(relative, k_in, v_in, halo, halo, conv_filter, lam_rows, res_rows)

    query = pl.pallas_call(
        functools.partial(query_kernel, rows=rows, genomes=genomes),
        grid_spec=pltpu.PrefetchScalarGridSpec(
            num_scalar_prefetch=1,
            grid=(steps,),
            in_specs=[stream, halo_spec(0), taps_spec],
            out_specs=stream,
            scratch_shapes=[pltpu.VMEM((1, 8, rows + 8, LANES), F32)],
        ),
        out_shape=jax.ShapeDtypeStruct((rows, width), BF16),
        name="query",
        cost_estimate=pl.CostEstimate(
            flops=6 * 10**9, bytes_accessed=5 * rows * width, transcendentals=0
        ),
    )(relative, q_in, halo, conv_filter)

    def end_id(device):
        return jnp.sum((starts <= (device + 1) * rows - 1).astype(jnp.int32))

    def joined(a, b):
        return (end_id(a) == end_id(b)).astype(F32)

    core = index % 2
    half = width // 2

    def mine_of(value):
        return lax.dynamic_slice_in_dim(value, core * half, half, 1)

    lam_mine = mine_of(lam_wide)

    def power(devices):
        return jnp.exp(-lam_mine * (rows * devices).astype(F32))

    def crossed(value, step, only=None):
        pairs = [(i, i ^ step) for i in range(count) if only is None or i // only % 4 in (1, 2)]
        return exchange(value.astype(BF16), pairs).astype(F32)

    one = jnp.int32(1)
    own = mine_of(span)
    got = mine_of(exchange(span, [(i, i ^ 1) for i in range(count)]))
    left = jnp.where(core == 0, own, got)
    right = jnp.where(core == 0, got, own)
    chip = index - core
    total = power(one) * joined(chip, chip + 1) * left + right
    prefix = jnp.zeros_like(total)
    size = 2
    while size * 4 < count or size * 2 == count:
        other = crossed(total, size)
        is_right = (index // size) % 2 == 1
        first = index // size * size
        last = first + size - 1
        into = power(chip - first) * joined(first - 1, chip - 1) * other
        prefix = prefix + jnp.where(is_right, into, 0.0)
        gain = power(jnp.int32(size))
        as_right = gain * joined(first - 1, last) * other + total
        as_left = gain * joined(last, last + size) * total + other
        total = jnp.where(is_right, as_right, as_left)
        size *= 2
    if size * 4 == count:
        block_index = index // size
        for flip, other in (
            (1, crossed(total, size)),
            (3, crossed(total, 3 * size, size)),
            (2, crossed(total, 2 * size)),
        ):
            source = block_index ^ flip
            after = (source + 1) * size
            factor = jnp.where(source < block_index, joined(after - 1, chip - 1), 0.0)
            prefix = prefix + power(jnp.maximum(chip - after, 0)) * factor * other
    second = power(one) * joined(chip - 1, chip) * prefix + left
    mine = jnp.where(core == 0, prefix, second)
    others = jnp.where(core == 0, second, prefix)
    back = exchange(others, [(i, i ^ 1) for i in range(count)])

    groups = width // (2 * LANES)
    flat_spec = pl.BlockSpec((groups // steps, 1, 2 * LANES), lambda b, *_: (b, 0, 0))
    half_spec = pl.BlockSpec((POLES, block), lambda b, *_: (0, b % (steps // 2)))
    return pl.pallas_call(
        functools.partial(gate_kernel, rows=rows, genomes=genomes),
        grid_spec=pltpu.PrefetchScalarGridSpec(
            num_scalar_prefetch=2,
            grid=(steps,),
            in_specs=[local_spec, stream, half_spec, half_spec, flat_spec, flat_spec],
            out_specs=stream,
        ),
        out_shape=jax.ShapeDtypeStruct((rows, width), BF16),
        name="gate",
    )(
        relative, jnp.reshape(core, (1,)).astype(jnp.int32), local, query, mine, back,
        decay_rate.reshape(groups, 1, 2 * LANES), residue.reshape(groups, 1, 2 * LANES),
    )


def solution(mesh):
    in_specs = (
        P(("groups", "ctx"), None),
        P(("groups", "ctx"), None),
        P(("groups", "ctx"), None),
        P(),
        P(),
        P(),
        P("groups"),
    )
    return jax.shard_map(
        per_device, mesh=mesh, in_specs=in_specs, out_specs=P(("groups", "ctx"), None), check_vma=False
    )
```

time: 409 us -> 68.9 us (0.17)
  the two profiles are of different devices: /device:TPU:18 before, /device:TPU:0 now
where the time goes in v2:
time: 68.9 us; the launch traced here: 69.3 us
  Pallas kernels  34.2 us (50%)
  starting transfers between devices  15.5 us (22%)
  between operations  10.1 us (15%)
  local copies, waits for them, and re-layouts  4.68 us (7%)
  other arithmetic  4 us (6%)
  waiting for transfers between devices  0.82 us (1%)
    pallas_call x1, Pallas kernels, per_device(): pl.pallas_call(functools.partial(states_kernel, rows=rows, genomes=genome...  19.1 us
    ppermute x7, starting transfers between devices, exchange(): return lax.ppermute(value, 'ctx', pairs)  15.5 us
    pallas_call x1, Pallas kernels, per_device(): pl.pallas_call(functools.partial(gate_kernel, rows=rows, genomes=genomes)...  6.74 us
    pallas_call x1, Pallas kernels, per_device(): pl.pallas_call(functools.partial(query_kernel, rows=rows, genomes=genomes...  6.27 us
    pallas_call x1, Pallas kernels, per_device(): pl.pallas_call(functools.partial(expand_kernel, tiles=tiles), out_shape=[...  2.11 us
    another operation x2, local copies, waits for them, and re-layouts, per_device(): tail = jnp.stack([x[rows - 8:] for x in (q_in, k_in, v_in)])  1.72 us
    unnamed x14, local copies, waits for them, and re-layouts  1.53 us
  transfers between devices with their start and end apart: 7, of which 2 were waited for; matrix products, arithmetic and copies ran while one was open for 6% of the time, Pallas kernels for 12%

profile of v2, /device:TPU:0, one launch (start us, length us, event | category | flops | bytes accessed | tf_op | source)
XLA Modules:
  0.0 69.3 jit_solution(17253365955848501119)
XLA Ops:
  0.0 0.8 %slice_bitcast_fusion.2 = bf16[1,8,4096]{2,1,0:T(8,128)(2,1)S(1)} fusion(bf16[256,4096]{1,0:T(8,128)(2,1)} %q_ref.1), kind=kLoop, calls=%fused_computation.20 | loop fusion | bytes 131072 | tf_op jit(solution)/shard_map/stack | solution.py:270
  0.8 0.9 %slice_bitcast_fusion = (bf16[1,8,4096]{2,1,0:T(8,128)(2,1)S(1)}, bf16[1,8,4096]{2,1,0:T(8,128)(2,1)S(1)}) fusion(bf16[256,4096]{1,0:T(8,128)(2,1)} %v_ref.1, bf16[256,4096]{1,0:T(8,128)(2,1)} %k_ref.1), kind=kLoop, calls=%fused_computation.18 | loop fusion | bytes 262144 | tf_op jit(solution)/shard_map/stack | solution.py:270
  1.8 2.4 %collective-permute-start = (bf16[3,8,4096]{2,1,0:T(8,128)(2,1)S(1)}, bf16[3,8,4096]{2,1,0:T(8,128)(2,1)S(1)}, u32[]{:S(2)}, u32[]{:S(2)}) collective-permute-start(bf16[3,8,4096]{2,1,0:T(8,128)(2,1)S(1)} %pad_maximum_fusion), channel_id=1, source_target_pairs={{0,1},{1,2},{2,3},{3,4},{4,5},{5,6},{6,7},{7,8},{8,9},{9,10},{10,1... | collective-permute-start | bytes 589832 | tf_op jit(solution)/shard_map/ppermute | solution.py:257
  4.2 0.8 %select_reduce_fusion = s32[4]{0:T(128)S(1)} fusion(s32[4]{0:T(128)} %param.13), kind=kLoop, calls=%fused_computation.21 | loop fusion | flops 44 | bytes 32 | tf_op jit(solution)/shard_map/reduce_sum | solution.py:267
  5.0 2.1 %expand.1 = (f32[16,32,128]{2,1,0:T(8,128)}, f32[16,32,128]{2,1,0:T(8,128)}, f32[16,4096]{1,0:T(8,128)}) custom-call(f32[16,256]{1,0:T(8,128)} %bitcast.9, f32[16,256]{1,0:T(8,128)} %bitcast.10), custom_call_target="tpu_custom_call" | custom-call | flops 1000000000 | bytes 1000000 | tf_op jit(solution)/shard_map/expand/pallas_call | solution.py:284
  7.1 1.3 %fusion.13 = (s32[]{:T(128)}, s32[]{:T(128)}, s32[]{:T(128)}, s32[]{:T(128)}, s32[]{:T(128)}, /*index=5*/s32[]{:T(128)}, s32[]{:T(128)}, s32[]{:T(128)}, s32[]{:T(128)}, s32[4]{0:T(128)}) fusion(s32[4]{0:T(128)S(1)} %select_reduce_fusion, s32[]{:T(128)S(6)} %sub.85, s32[]{:T(128)S(6)} %sub.91, s32[]{:T(128)S(6)} %sub.89, s32[]{:T(128)S(6)} %sub.87, ...), kind=kLoop, calls=%fused_computation.36 | loop fusion | flops 103 | bytes 108 | tf_op jit(solution)/shard_map/reduce_sum | solution.py:331
  8.4 0.0 collective-permute-done.k_halo.v_halo.q_halo
  8.4 0.7 copy-done.1
  9.1 19.1 %states.1 = (f32[32,256,128]{2,1,0:T(8,128)}, f32[16,4096]{1,0:T(8,128)}) custom-call(s32[4]{0:T(128)} %get-tuple-element.28.starts, bf16[256,4096]{1,0:T(8,128)(2,1)} %k_ref.1, bf16[256,4096]{1,0:T(8,128)(2,1)} %v_ref.1, bf16[3,8,4096]{2,1,0:T(8,128)(2,1)} %copy-done.1, bf16[3,8,4096]{2,1,0:T(8,128)(2,1)} %copy-done.1, f32[3,7,4096]{2,1,0:T(8,128)} %taps_ref.3, ...), custom_call_target="tpu_custom_call" | custom-call | tf_op jit(solution)/shard_map/states/pallas_call | solution.py:295
  28.2 2.6 %collective-permute-start.1 = (f32[16,4096]{1,0:T(8,128)}, f32[16,4096]{1,0:T(8,128)S(1)}, u32[]{:S(2)}, u32[]{:S(2)}) collective-permute-start(f32[16,4096]{1,0:T(8,128)} %get-tuple-element.14), channel_id=1, source_target_pairs={{0,1},{1,0},{2,3},{3,2},{4,5},{5,4},{6,7},{7,6},{8,9},{9,8},{10,11... | collective-permute-start | bytes 786440 | tf_op jit(solution)/shard_map/ppermute | solution.py:257
  32.0 0.2 collective-permute-done.1
  32.2 1.0 %fusion.19 = (bf16[16,2048]{1,0:T(8,128)(2,1)S(1)}, f32[16,2048]{1,0:T(8,128)S(1)}) fusion(f32[16,4096]{1,0:T(8,128)S(1)} %collective-permute-done.1, s32[]{:T(128)S(6)} %select_n.76, f32[16,4096]{1,0:T(8,128)} %get-tuple-element.14, pred[]{:T(512)S(6)} %eq.36, f32[]{:T(128)S(6)} %convert_element_type.96, f32[16,4096]{1,0:T(8,128)S(1)} %copy-done), kind=kLoop, calls=%fused_computation.42 | loop fusion | flops 262144 | bytes 589833 | tf_op jit(solution)/shard_map/convert_element_type | solution.py:349
  33.1 1.6 %collective-permute-start.2 = (bf16[16,2048]{1,0:T(8,128)(2,1)S(1)}, bf16[16,2048]{1,0:T(8,128)(2,1)S(1)}, u32[]{:S(2)}, u32[]{:S(2)}) collective-permute-start(bf16[16,2048]{1,0:T(8,128)(2,1)S(1)} %get-tuple-element.26), channel_id=1, source_target_pairs={{0,2},{1,3},{2,0},{3,1},{4,6},{5,7},{6,4},{7,5},{8,10},{9,11},{10,... | collective-permute-start | bytes 196616 | tf_op jit(solution)/shard_map/ppermute | solution.py:257
  34.7 0.1 copy.14
  34.8 0.1 copy.15
  43.7 0.7 %reshape.13.lam_ref = f32[16,1,256]{2,1,0:T(1,128)} reshape(f32[256,16]{1,0:T(8,128)S(1)} %copy.14) | data formatting | bytes 32768 | tf_op jit(solution)/shard_map/reshape | solution.py:403
  44.4 0.7 %reshape.14.res_ref = f32[16,1,256]{2,1,0:T(1,128)} reshape(f32[256,16]{1,0:T(8,128)S(1)} %copy.15) | data formatting | bytes 32768 | tf_op jit(solution)/shard_map/reshape | solution.py:403
  45.1 0.0 collective-permute-done.2
  45.1 0.1 fusion.6
  45.2 6.3 %collective-permute-start.5 = (bf16[16,2048]{1,0:T(8,128)(2,1)S(1)}, bf16[16,2048]{1,0:T(8,128)(2,1)S(1)}, u32[]{:S(2)}, u32[]{:S(2)}) collective-permute-start(bf16[16,2048]{1,0:T(8,128)(2,1)S(1)} %fusion.6), channel_id=1, source_target_pairs={{0,8},{1,9},{2,10},{3,11},{4,12},{5,13},{6,14},{7,15},{8,0},{9,1},... | collective-permute-start | bytes 196616 | tf_op jit(solution)/shard_map/ppermute | solution.py:257
  51.5 0.7 collective-permute-start.4
  52.1 1.9 %collective-permute-start.3 = (bf16[16,2048]{1,0:T(8,128)(2,1)S(1)}, bf16[16,2048]{1,0:T(8,128)(2,1)S(1)}, u32[]{:S(2)}, u32[]{:S(2)}) collective-permute-start(bf16[16,2048]{1,0:T(8,128)(2,1)S(1)} %fusion.6), channel_id=1, source_target_pairs={{0,4},{1,5},{2,6},{3,7},{4,0},{5,1},{6,2},{7,3},{8,12},{9,13},{10,... | collective-permute-start | bytes 196616 | tf_op jit(solution)/shard_map/ppermute | solution.py:257
  54.0 6.3 %query.1.query_ref = bf16[256,4096]{1,0:T(8,128)(2,1)} custom-call(s32[4]{0:T(128)} %get-tuple-element.28.starts, bf16[256,4096]{1,0:T(8,128)(2,1)} %q_ref.1, bf16[3,8,4096]{2,1,0:T(8,128)(2,1)} %copy-done.1, f32[3,7,4096]{2,1,0:T(8,128)} %taps_ref.3), custom_call_target="tpu_custom_call" | custom-call | flops 6000000000 | bytes 5242880 | tf_op jit(solution)/shard_map/query/pallas_call | solution.py:314
  60.3 0.0 collective-permute-done.5
  60.3 0.0 collective-permute-done.4
  60.3 0.0 collective-permute-done.3
  60.3 0.2 fusion.7
  60.5 0.1 collective-permute-start.6
  60.6 0.7 %fusion.8.mine_ref = f32[16,2048]{1,0:T(8,128)} fusion(f32[16,2048]{1,0:T(8,128)S(1)} %get-tuple-element.25, f32[16,4096]{1,0:T(8,128)S(1)} %copy-done, s32[]{:T(128)S(6)} %select_n.76, f32[]{:T(128)S(6)} %convert_element_type.116, pred[]{:T(512)S(6)} %eq.36, f32[16,4096]{1,0:T(8,128)S(1)} %collective-permute-done.1, f32[16,4096]{1,0:T(8,128)S(1)} %copy-done.2), kind=kLoop, calls=%fused_computation.17 | loop fusion | flops 229376 | bytes 655369 | tf_op jit(solution)/shard_map/jit(_where)/select_n | solution.py:384
  61.3 0.6 collective-permute-done.6.other_ref
  61.9 0.6 copy-done.3
  62.6 6.7 %gate.1 = bf16[256,4096]{1,0:T(8,128)(2,1)} custom-call(s32[4]{0:T(128)} %get-tuple-element.28.starts, s32[1]{0:T(128)} %bitcast.core_ref, f32[32,256,128]{2,1,0:T(8,128)} %get-tuple-element.12.local_ref, bf16[256,4096]{1,0:T(8,128)(2,1)} %query.1.query_ref, f32[16,2048]{1,0:T(8,128)} %fusion.8.mine_ref, f32[16,2048]{1,0:T(8,128)} %copy-done.3, ...), custom_call_target="tpu_custom_call" | custom-call | tf_op jit(solution)/shard_map/gate/pallas_call | solution.py:391
  (11 shorter events, 0.0 us)
Async XLA Ops:
  1.8 6.7 %collective-permute-start = (bf16[3,8,4096]{2,1,0:T(8,128)(2,1)S(1)}, bf16[3,8,4096]{2,1,0:T(8,128)(2,1)S(1)}, u32[]{:S(2)}, u32[]{:S(2)}) collective-permute-start(bf16[3,8,4096]{2,1,0:T(8,128)(2,1)S(1)} %pad_maximum_fusion), channel_id=1, source_target_pairs={{0,1},{1,2},{2,3},{3,4},{4,5},{5,6},{6,7},{7,8},{8,9},{9,10},{10,1... | collective-permute-start | bytes 589832 | tf_op jit(solution)/shard_map/ppermute | solution.py:257
  8.4 0.7 copy-start.1
  9.1 23.1 %copy-start = (f32[16,4096]{1,0:T(8,128)S(1)}, f32[16,4096]{1,0:T(8,128)}, u32[]{:S(2)}) copy-start(f32[16,4096]{1,0:T(8,128)} %get-tuple-element.13) | copy-start | bytes 786436
  9.1 25.6 %copy-start.4 = (f32[256,16]{0,1:T(8,128)S(1)}, f32[256,16]{0,1:T(8,128)}, u32[]{:S(2)}) copy-start(f32[256,16]{0,1:T(8,128)} %param.11) | copy-start | bytes 49156
  9.1 25.7 %copy-start.5 = (f32[256,16]{0,1:T(8,128)S(1)}, f32[256,16]{0,1:T(8,128)}, u32[]{:S(2)}) copy-start(f32[256,16]{0,1:T(8,128)} %param.12) | copy-start | bytes 49156
  28.2 4.0 %collective-permute-start.1 = (f32[16,4096]{1,0:T(8,128)}, f32[16,4096]{1,0:T(8,128)S(1)}, u32[]{:S(2)}, u32[]{:S(2)}) collective-permute-start(f32[16,4096]{1,0:T(8,128)} %get-tuple-element.14), channel_id=1, source_target_pairs={{0,1},{1,0},{2,3},{3,2},{4,5},{5,4},{6,7},{7,6},{8,9},{9,8},{10,11... | collective-permute-start | bytes 786440 | tf_op jit(solution)/shard_map/ppermute | solution.py:257
  33.1 12.0 %collective-permute-start.2 = (bf16[16,2048]{1,0:T(8,128)(2,1)S(1)}, bf16[16,2048]{1,0:T(8,128)(2,1)S(1)}, u32[]{:S(2)}, u32[]{:S(2)}) collective-permute-start(bf16[16,2048]{1,0:T(8,128)(2,1)S(1)} %get-tuple-element.26), channel_id=1, source_target_pairs={{0,2},{1,3},{2,0},{3,1},{4,6},{5,7},{6,4},{7,5},{8,10},{9,11},{10,... | collective-permute-start | bytes 196616 | tf_op jit(solution)/shard_map/ppermute | solution.py:257
  45.2 15.1 %copy-start.2 = (f32[16,4096]{1,0:T(8,128)S(1)}, f32[16,4096]{1,0:T(8,128)}, u32[]{:S(2)}) copy-start(f32[16,4096]{1,0:T(8,128)} %get-tuple-element.14) | copy-start | bytes 786436
  45.2 15.1 %collective-permute-start.5 = (bf16[16,2048]{1,0:T(8,128)(2,1)S(1)}, bf16[16,2048]{1,0:T(8,128)(2,1)S(1)}, u32[]{:S(2)}, u32[]{:S(2)}) collective-permute-start(bf16[16,2048]{1,0:T(8,128)(2,1)S(1)} %fusion.6), channel_id=1, source_target_pairs={{0,8},{1,9},{2,10},{3,11},{4,12},{5,13},{6,14},{7,15},{8,0},{9,1},... | collective-permute-start | bytes 196616 | tf_op jit(solution)/shard_map/ppermute | solution.py:257
  51.5 8.8 %collective-permute-start.4 = (bf16[16,2048]{1,0:T(8,128)(2,1)S(1)}, bf16[16,2048]{1,0:T(8,128)(2,1)S(1)}, u32[]{:S(2)}, u32[]{:S(2)}) collective-permute-start(bf16[16,2048]{1,0:T(8,128)(2,1)S(1)} %fusion.6), channel_id=1, source_target_pairs={{4,8},{5,9},{6,10},{7,11},{8,4},{9,5},{10,6},{11,7},{20,24},{21,25... | collective-permute-start | bytes 196616 | tf_op jit(solution)/shard_map/ppermute | solution.py:257
  52.1 8.2 %collective-permute-start.3 = (bf16[16,2048]{1,0:T(8,128)(2,1)S(1)}, bf16[16,2048]{1,0:T(8,128)(2,1)S(1)}, u32[]{:S(2)}, u32[]{:S(2)}) collective-permute-start(bf16[16,2048]{1,0:T(8,128)(2,1)S(1)} %fusion.6), channel_id=1, source_target_pairs={{0,4},{1,5},{2,6},{3,7},{4,0},{5,1},{6,2},{7,3},{8,12},{9,13},{10,... | collective-permute-start | bytes 196616 | tf_op jit(solution)/shard_map/ppermute | solution.py:257
  60.5 1.4 %collective-permute-start.6 = (f32[16,2048]{1,0:T(8,128)S(1)}, f32[16,2048]{1,0:T(8,128)S(1)}, u32[]{:S(2)}, u32[]{:S(2)}) collective-permute-start(f32[16,2048]{1,0:T(8,128)S(1)} %get-tuple-element.24), channel_id=1, source_target_pairs={{0,1},{1,0},{2,3},{3,2},{4,5},{5,4},{6,7},{7,6},{8,9},{9,8},{10,11... | collective-permute-start | bytes 393224 | tf_op jit(solution)/shard_map/ppermute | solution.py:257
  61.9 0.7 copy-start.3

commit v3 on v2

--- a/solution.py
+++ b/solution.py
@@ -116,7 +116,62 @@
             patch(end)
 
 
-def expand_kernel(lam_ref, res_ref, lam_rows, res_rows, lam_wide, *, tiles):
+def exchange_plan(count):
+    sizes, size = [], 2
+    while size * 4 < count or size * 2 == count:
+        sizes.append(size)
+        size *= 2
+    return sizes, size if size * 4 == count else 0
+
+
+FLIPS = (1, 3, 2)
+
+
+def factors(lengths, index, count, rows, genomes):
+    starts = [jnp.int32(0)]
+    for g in range(1, genomes):
+        starts.append(starts[-1] + lengths[g - 1])
+
+    def joined(a, b):
+        cut = any_of(
+            [(start >= (a + 1) * rows) & (start < (b + 1) * rows) for start in starts]
+        )
+        return jnp.where(cut, 0.0, 1.0)
+
+    core = lax.rem(index, 2)
+    chip = index - core
+    out = [(jnp.int32(1), joined(chip, chip + 1))]
+    sizes, wide = exchange_plan(count)
+    for size in sizes:
+        right = lax.rem(lax.div(index, size), 2) == 1
+        first = lax.div(index, size) * size
+        last = first + size - 1
+        out.append((chip - first, jnp.where(right, joined(first - 1, chip - 1), 0.0)))
+        out.append((jnp.where(right, size, 0), jnp.where(right, joined(first - 1, last), 1.0)))
+        out.append((jnp.where(right, 0, size), jnp.where(right, 1.0, joined(last, last + size))))
+    if wide:
+        block = lax.div(index, wide)
+        for flip in FLIPS:
+            source = block ^ flip
+            after = (source + 1) * wide
+            out.append(
+                (
+                    jnp.maximum(chip - after, 0),
+                    jnp.where(source < block, joined(after - 1, chip - 1), 0.0),
+                )
+            )
+    out.append((jnp.int32(1), joined(chip - 1, chip)))
+    return [start - index * rows for start in starts], out, core
+
+
+def expand_kernel(
+    lengths, lam_ref, res_ref, starts_ref, lam_rows, res_rows, factor_ref, lam_mine,
+    *, tiles, count, rows, genomes,
+):
+    index = lax.axis_index("ctx")
+    starts, pairs, core = factors(lengths, index, count, rows, genomes)
+    for g in range(genomes):
+        starts_ref[g] = starts[g]
     parts = []
     for source in (lam_ref, res_ref):
         rest = source[...]
@@ -125,6 +180,7 @@
             rest = rest - part.astype(F32)
             parts.append(part)
     parts = jnp.concatenate(parts, 0)
+    lams = []
     for pair in range(tiles // 2):
         first = pair * 2 * GROUP
         side = first // LANES * LANES
@@ -137,10 +193,16 @@
         wide = [wide[i * POLES : (i + 1) * POLES] for i in range(6)]
         lam = wide[0] + wide[1] + wide[2]
         res = wide[3] + wide[4] + wide[5]
-        lam_wide[:, 2 * pair * LANES : (2 * pair + 2) * LANES] = lam
+        half = pl.ds(pair % (tiles // 4) * 2 * LANES, 2 * LANES)
+        if pair < tiles // 4:
+            lam_mine[:, half] = lam
+        else:
+            lam_mine[:, half] = jnp.where(core == 0, lam_mine[:, half], lam)
         for t in range(2):
             lam_rows[:, 2 * pair + t, :] = lam[:, lanes_of(t)]
             res_rows[:, 2 * pair + t, :] = res[:, lanes_of(t)]
+    for i, (devices, factor) in enumerate(pairs):
+        factor_ref[i] = factor * jnp.exp(-lam_mine[...] * (devices * rows).astype(F32))
 
 
 def states_kernel(
@@ -263,10 +325,6 @@
     genomes = genome_lengths.shape[0]
     count = lax.axis_size("ctx")
     index = lax.axis_index("ctx")
-    order = jnp.arange(genomes)
-    starts = jnp.sum(jnp.where(order[None, :] < order[:, None], genome_lengths[None, :], 0), 1)
-    relative = (starts - index * rows).astype(jnp.int32)
-
     tail = jnp.stack([x[rows - 8 :] for x in (q_in, k_in, v_in)])
     halo = exchange(tail, [(i, i + 1) for i in range(count - 1)])
 
@@ -281,16 +339,24 @@
     def halo_spec(s):
         return pl.BlockSpec((1, 8, block), lambda b, *_: (s, 0, b))
 
-    lam_rows, res_rows, lam_wide = pl.pallas_call(
-        functools.partial(expand_kernel, tiles=tiles),
+    in_smem = pl.BlockSpec(memory_space=pltpu.SMEM)
+    in_vmem = pl.BlockSpec(memory_space=pltpu.VMEM)
+    sizes, wide = exchange_plan(count)
+    terms = 2 + 3 * len(sizes) + (len(FLIPS) if wide else 0)
+    relative, lam_rows, res_rows, factor = pl.pallas_call(
+        functools.partial(expand_kernel, tiles=tiles, count=count, rows=rows, genomes=genomes),
+        in_specs=[in_smem, in_vmem, in_vmem],
+        out_specs=[in_smem] + [in_vmem] * 3,
         out_shape=[
+            jax.ShapeDtypeStruct((genomes,), jnp.int32),
             jax.ShapeDtypeStruct((POLES, tiles, LANES), F32),
             jax.ShapeDtypeStruct((POLES, tiles, LANES), F32),
-            jax.ShapeDtypeStruct((POLES, width), F32),
+            jax.ShapeDtypeStruct((terms, POLES, width // 2), F32),
         ],
+        scratch_shapes=[pltpu.VMEM((POLES, width // 2), F32)],
         name="expand",
         cost_estimate=pl.CostEstimate(flops=10**9, bytes_accessed=10**6, transcendentals=0),
-    )(decay_rate.T, residue.T)
+    )(genome_lengths, decay_rate.T, residue.T)
 
     local, span = pl.pallas_call(
         functools.partial(states_kernel, rows=rows, genomes=genomes),
@@ -327,60 +393,39 @@
         ),
     )(relative, q_in, halo, conv_filter)
 
-    def end_id(device):
-        return jnp.sum((starts <= (device + 1) * rows - 1).astype(jnp.int32))
-
-    def joined(a, b):
-        return (end_id(a) == end_id(b)).astype(F32)
-
     core = index % 2
     half = width // 2
 
     def mine_of(value):
         return lax.dynamic_slice_in_dim(value, core * half, half, 1)
 
-    lam_mine = mine_of(lam_wide)
-
-    def power(devices):
-        return jnp.exp(-lam_mine * (rows * devices).astype(F32))
+    def term(i, value):
+        return factor[i] * value
 
     def crossed(value, step, only=None):
         pairs = [(i, i ^ step) for i in range(count) if only is None or i // only % 4 in (1, 2)]
-        return exchange(value.astype(BF16), pairs).astype(F32)
-
-    one = jnp.int32(1)
+        return exchange(value, pairs).astype(F32)
+
     own = mine_of(span)
     got = mine_of(exchange(span, [(i, i ^ 1) for i in range(count)]))
     left = jnp.where(core == 0, own, got)
     right = jnp.where(core == 0, got, own)
-    chip = index - core
-    total = power(one) * joined(chip, chip + 1) * left + right
+    total = term(0, left) + right
     prefix = jnp.zeros_like(total)
-    size = 2
-    while size * 4 < count or size * 2 == count:
-        other = crossed(total, size)
-        is_right = (index // size) % 2 == 1
-        first = index // size * size
-        last = first + size - 1
-        into = power(chip - first) * joined(first - 1, chip - 1) * other
-        prefix = prefix + jnp.where(is_right, into, 0.0)
-        gain = power(jnp.int32(size))
-        as_right = gain * joined(first - 1, last) * other + total
-        as_left = gain * joined(last, last + size) * total + other
-        total = jnp.where(is_right, as_right, as_left)
-        size *= 2
-    if size * 4 == count:
-        block_index = index // size
-        for flip, other in (
-            (1, crossed(total, size)),
-            (3, crossed(total, 3 * size, size)),
-            (2, crossed(total, 2 * size)),
-        ):
-            source = block_index ^ flip
-            after = (source + 1) * size
-            factor = jnp.where(source < block_index, joined(after - 1, chip - 1), 0.0)
-            prefix = prefix + power(jnp.maximum(chip - after, 0)) * factor * other
-    second = power(one) * joined(chip - 1, chip) * prefix + left
+    at = 1
+    for size in sizes:
+        other = crossed(total.astype(BF16), size)
+        prefix = prefix + term(at, other)
+        total = term(at + 1, other) + term(at + 2, total)
+        at += 3
+    if wide:
+        sent = total.astype(BF16)
+        others = [crossed(sent, f * wide, wide if f == 3 else None) for f in FLIPS]
+        query, *others = lax.optimization_barrier((query, *others))
+        for other in others:
+            prefix = prefix + term(at, other)
+            at += 1
+    second = term(at, prefix) + left
     mine = jnp.where(core == 0, prefix, second)
     others = jnp.where(core == 0, second, prefix)
     back = exchange(others, [(i, i ^ 1) for i in range(count)])

time: 68.9 us -> 60.5 us (0.88); the launches traced: 69.3 us -> 59.4 us
  between operations: 10.1 us -> 0.14 us
  waiting for transfers between devices: 0.82 us -> 4.16 us
  other arithmetic: 4 us -> 1.77 us
  starting transfers between devices: 15.5 us -> 14.1 us
    ppermute x7, waiting for transfers between devices: 0.82 us -> 4.16 us  [exchange(): return lax.ppermute(value, 'ctx', pairs)]
    reduce_sum x2 -> x0, other arithmetic: 2.09 us -> none  [the longest x1 1.32 us: end_id(): return jnp.sum((starts <= (device + 1) * rows - 1).astype(jnp.int32))]
    ppermute x7, starting transfers between devices: 15.5 us -> 14.1 us  [exchange(): return lax.ppermute(value, 'ctx', pairs)]
  transfers between devices with their start and end apart: 7 -> 7, of which waited for: 2 -> 3; matrix products, arithmetic and copies ran while one was open for 6% -> 4% of each run, Pallas kernels for 12% -> 15%
where the time goes in v3:
time: 60.5 us; the launch traced here: 59.4 us
  Pallas kernels  34.6 us (57%)
  starting transfers between devices  14.1 us (23%)
  local copies, waits for them, and re-layouts  4.69 us (8%)
  waiting for transfers between devices  4.16 us (7%)
  other arithmetic  1.77 us (3%)
    pallas_call x1, Pallas kernels, per_device(): pl.pallas_call(functools.partial(states_kernel, rows=rows, genomes=genome...  19.1 us
    ppermute x7, starting transfers between devices, exchange(): return lax.ppermute(value, 'ctx', pairs)  14.1 us
    pallas_call x1, Pallas kernels, per_device(): pl.pallas_call(functools.partial(gate_kernel, rows=rows, genomes=genomes)...  6.74 us
    pallas_call x1, Pallas kernels, per_device(): pl.pallas_call(functools.partial(query_kernel, rows=rows, genomes=genomes...  6.25 us
    ppermute x7, waiting for transfers between devices, exchange(): return lax.ppermute(value, 'ctx', pairs)  4.16 us
    pallas_call x1, Pallas kernels, per_device(): pl.pallas_call(functools.partial(expand_kernel, tiles=tiles, count=count,...  2.53 us
    another operation x2, local copies, waits for them, and re-layouts, per_device(): tail = jnp.stack([x[rows - 8:] for x in (q_in, k_in, v_in)])  1.72 us
    unnamed x14, local copies, waits for them, and re-layouts  1.54 us
  transfers between devices with their start and end apart: 7, of which 3 were waited for; matrix products, arithmetic and copies ran while one was open for 4% of the time, Pallas kernels for 15%

profile of v3, /device:TPU:0, one launch (start us, length us, event | category | flops | bytes accessed | tf_op | source)
XLA Modules:
  0.0 59.4 jit_solution(11252393729190591806)
XLA Ops:
  0.0 0.8 %slice_bitcast_fusion.2 = bf16[1,8,4096]{2,1,0:T(8,128)(2,1)S(1)} fusion(bf16[256,4096]{1,0:T(8,128)(2,1)} %q_ref.1), kind=kLoop, calls=%fused_computation.21 | loop fusion | bytes 131072 | tf_op jit(solution)/shard_map/stack | solution.py:328
  0.8 0.9 %slice_bitcast_fusion = (bf16[1,8,4096]{2,1,0:T(8,128)(2,1)S(1)}, bf16[1,8,4096]{2,1,0:T(8,128)(2,1)S(1)}) fusion(bf16[256,4096]{1,0:T(8,128)(2,1)} %v_ref.1, bf16[256,4096]{1,0:T(8,128)(2,1)} %k_ref.1), kind=kLoop, calls=%fused_computation.19 | loop fusion | bytes 262144 | tf_op jit(solution)/shard_map/stack | solution.py:328
  1.8 2.4 %collective-permute-start = (bf16[3,8,4096]{2,1,0:T(8,128)(2,1)S(1)}, bf16[3,8,4096]{2,1,0:T(8,128)(2,1)S(1)}, u32[]{:S(2)}, u32[]{:S(2)}) collective-permute-start(bf16[3,8,4096]{2,1,0:T(8,128)(2,1)S(1)} %pad_maximum_fusion), channel_id=1, source_target_pairs={{0,1},{1,2},{2,3},{3,4},{4,5},{5,6},{6,7},{7,8},{8,9},{9,10},{10,1... | collective-permute-start | bytes 589832 | tf_op jit(solution)/shard_map/ppermute | solution.py:319
  4.2 2.5 %expand.1 = (s32[4]{0:T(128)}, f32[16,32,128]{2,1,0:T(8,128)}, f32[16,32,128]{2,1,0:T(8,128)}, f32[8,16,2048]{2,1,0:T(8,128)}) custom-call(s32[4]{0:T(128)} %lengths.1, f32[16,256]{1,0:T(8,128)} %bitcast.46, f32[16,256]{1,0:T(8,128)} %bitcast.47), custom_call_target="tpu_custom_call" | custom-call | flops 1000000000 | bytes 1000000 | tf_op jit(solution)/shard_map/expand/pallas_call | solution.py:346
  6.7 0.0 collective-permute-done.k_halo.v_halo.q_halo
  6.7 0.0 copy-start.1
  6.7 0.7 %copy-done.1 = bf16[3,8,4096]{2,1,0:T(8,128)(2,1)} copy-done((bf16[3,8,4096]{2,1,0:T(8,128)(2,1)}, bf16[3,8,4096]{2,1,0:T(8,128)(2,1)S(1)}, u32[]{:S(2)}) %copy-start.1) | copy-done | bytes 196632
  7.4 19.1 %states.1 = (f32[32,256,128]{2,1,0:T(8,128)}, f32[16,4096]{1,0:T(8,128)}) custom-call(s32[4]{0:T(128)} %get-tuple-element.15.starts, bf16[256,4096]{1,0:T(8,128)(2,1)} %k_ref.1, bf16[256,4096]{1,0:T(8,128)(2,1)} %v_ref.1, bf16[3,8,4096]{2,1,0:T(8,128)(2,1)} %copy-done.1, bf16[3,8,4096]{2,1,0:T(8,128)(2,1)} %copy-done.1, f32[3,7,4096]{2,1,0:T(8,128)} %taps_ref.3, ...), custom_call_target="tpu_custom_call" | custom-call | tf_op jit(solution)/shard_map/states/pallas_call | solution.py:361
  26.5 5.4 %collective-permute-start.1 = (f32[16,4096]{1,0:T(8,128)}, f32[16,4096]{1,0:T(8,128)S(1)}, u32[]{:S(2)}, u32[]{:S(2)}) collective-permute-start(f32[16,4096]{1,0:T(8,128)} %get-tuple-element.20), channel_id=1, source_target_pairs={{0,1},{1,0},{2,3},{3,2},{4,5},{5,4},{6,7},{7,6},{8,9},{9,8},{10,11... | collective-permute-start | bytes 786440 | tf_op jit(solution)/shard_map/ppermute | solution.py:319
  31.9 1.4 %collective-permute-done.1 = f32[16,4096]{1,0:T(8,128)S(1)} collective-permute-done((f32[16,4096]{1,0:T(8,128)}, f32[16,4096]{1,0:T(8,128)S(1)}, u32[]{:S(2)}, u32[]{:S(2)}) %collective-permute-start.1) | collective-permute-done | bytes 262176 | tf_op jit(solution)/shard_map/ppermute | solution.py:319
  33.2 0.9 %fusion.10 = (bf16[16,2048]{1,0:T(8,128)(2,1)S(1)}, f32[16,2048]{1,0:T(8,128)S(1)}) fusion(f32[16,4096]{1,0:T(8,128)S(1)} %collective-permute-done.1, s32[]{:T(128)S(6)} %select_n.33, f32[16,4096]{1,0:T(8,128)} %get-tuple-element.20, pred[]{:T(512)S(6)} %eq.4, f32[8,16,2048]{2,1,0:T(8,128)S(1)} %copy-done), kind=kLoop, calls=%fused_computation.22 | loop fusion | flops 163840 | bytes 589829 | tf_op jit(solution)/shard_map/convert_element_type | solution.py:417
  34.2 0.7 %collective-permute-start.2 = (bf16[16,2048]{1,0:T(8,128)(2,1)S(1)}, bf16[16,2048]{1,0:T(8,128)(2,1)S(1)}, u32[]{:S(2)}, u32[]{:S(2)}) collective-permute-start(bf16[16,2048]{1,0:T(8,128)(2,1)S(1)} %get-tuple-element.27), channel_id=1, source_target_pairs={{0,2},{1,3},{2,0},{3,1},{4,6},{5,7},{6,4},{7,5},{8,10},{9,11},{10,... | collective-permute-start | bytes 196616 | tf_op jit(solution)/shard_map/ppermute | solution.py:319
  34.9 0.1 copy.10
  35.0 0.0 copy-done.5
  35.0 0.1 copy.11
  35.1 0.7 %reshape.12.lam_ref = f32[16,1,256]{2,1,0:T(1,128)} reshape(f32[256,16]{1,0:T(8,128)S(1)} %copy.10) | data formatting | bytes 32768 | tf_op jit(solution)/shard_map/reshape | solution.py:448
  35.8 0.7 %reshape.13.res_ref = f32[16,1,256]{2,1,0:T(1,128)} reshape(f32[256,16]{1,0:T(8,128)S(1)} %copy.11) | data formatting | bytes 32768 | tf_op jit(solution)/shard_map/reshape | solution.py:448
  36.5 2.1 %collective-permute-done.2 = bf16[16,2048]{1,0:T(8,128)(2,1)S(1)} collective-permute-done((bf16[16,2048]{1,0:T(8,128)(2,1)S(1)}, bf16[16,2048]{1,0:T(8,128)(2,1)S(1)}, u32[]{:S(2)}, u32[]{:S(2)}) %collective-permute-start.2) | collective-permute-done | bytes 65568 | tf_op jit(solution)/shard_map/ppermute | solution.py:319
  38.7 1.9 %collective-permute-start.5 = (bf16[16,2048]{1,0:T(8,128)(2,1)S(1)}, bf16[16,2048]{1,0:T(8,128)(2,1)S(1)}, u32[]{:S(2)}, u32[]{:S(2)}) collective-permute-start(bf16[16,2048]{1,0:T(8,128)(2,1)S(1)} %fusion.1), channel_id=1, source_target_pairs={{0,8},{1,9},{2,10},{3,11},{4,12},{5,13},{6,14},{7,15},{8,0},{9,1},... | collective-permute-start | bytes 196616 | tf_op jit(solution)/shard_map/ppermute | solution.py:319
  40.6 0.7 %collective-permute-start.4 = (bf16[16,2048]{1,0:T(8,128)(2,1)S(1)}, bf16[16,2048]{1,0:T(8,128)(2,1)S(1)}, u32[]{:S(2)}, u32[]{:S(2)}) collective-permute-start(bf16[16,2048]{1,0:T(8,128)(2,1)S(1)} %fusion.1), channel_id=1, source_target_pairs={{4,8},{5,9},{6,10},{7,11},{8,4},{9,5},{10,6},{11,7},{20,24},{21,25... | collective-permute-start | bytes 196616 | tf_op jit(solution)/shard_map/ppermute | solution.py:319
  41.3 2.9 %collective-permute-start.3 = (bf16[16,2048]{1,0:T(8,128)(2,1)S(1)}, bf16[16,2048]{1,0:T(8,128)(2,1)S(1)}, u32[]{:S(2)}, u32[]{:S(2)}) collective-permute-start(bf16[16,2048]{1,0:T(8,128)(2,1)S(1)} %fusion.1), channel_id=1, source_target_pairs={{0,4},{1,5},{2,6},{3,7},{4,0},{5,1},{6,2},{7,3},{8,12},{9,13},{10,... | collective-permute-start | bytes 196616 | tf_op jit(solution)/shard_map/ppermute | solution.py:319
  44.2 6.3 %query.1.query_ref = bf16[256,4096]{1,0:T(8,128)(2,1)} custom-call(s32[4]{0:T(128)} %get-tuple-element.15.starts, bf16[256,4096]{1,0:T(8,128)(2,1)} %q_ref.1, bf16[3,8,4096]{2,1,0:T(8,128)(2,1)} %copy-done.1, f32[3,7,4096]{2,1,0:T(8,128)} %taps_ref.3), custom_call_target="tpu_custom_call" | custom-call | flops 6000000000 | bytes 5242880 | tf_op jit(solution)/shard_map/query/pallas_call | solution.py:380
  50.4 0.0 collective-permute-done.5
  50.5 0.0 collective-permute-done.4
  50.5 0.0 collective-permute-done.3
  50.5 0.0 copy-done.2
  50.5 0.1 fusion.7
  50.6 0.1 collective-permute-start.6
  50.7 0.7 %fusion.8.mine_ref = f32[16,2048]{1,0:T(8,128)} fusion(f32[16,2048]{1,0:T(8,128)S(1)} %get-tuple-element.26, f32[8,16,2048]{2,1,0:T(8,128)S(1)} %copy-done, pred[]{:T(512)S(6)} %eq.4, f32[16,4096]{1,0:T(8,128)S(1)} %collective-permute-done.1, s32[]{:T(128)S(6)} %select_n.33, f32[16,4096]{1,0:T(8,128)S(1)} %copy-done.2), kind=kLoop, calls=%fused_computation.18 | loop fusion | flops 131072 | bytes 655365 | tf_op jit(solution)/shard_map/jit(_where)/select_n | solution.py:429
  51.4 0.7 %collective-permute-done.6.other_ref = f32[16,2048]{1,0:T(8,128)S(1)} collective-permute-done((f32[16,2048]{1,0:T(8,128)S(1)}, f32[16,2048]{1,0:T(8,128)S(1)}, u32[]{:S(2)}, u32[]{:S(2)}) %collective-permute-start.6) | collective-permute-done | bytes 131104 | tf_op jit(solution)/shard_map/ppermute | solution.py:319
  52.0 0.7 %copy-done.3 = f32[16,2048]{1,0:T(8,128)} copy-done((f32[16,2048]{1,0:T(8,128)}, f32[16,2048]{1,0:T(8,128)S(1)}, u32[]{:S(2)}) %copy-start.3) | copy-done | bytes 131096
  52.7 6.7 %gate.1 = bf16[256,4096]{1,0:T(8,128)(2,1)} custom-call(s32[4]{0:T(128)} %get-tuple-element.15.starts, s32[1]{0:T(128)} %bitcast.2.core_ref, f32[32,256,128]{2,1,0:T(8,128)} %get-tuple-element.18.local_ref, bf16[256,4096]{1,0:T(8,128)(2,1)} %query.1.query_ref, f32[16,2048]{1,0:T(8,128)} %fusion.8.mine_ref, f32[16,2048]{1,0:T(8,128)} %copy-done.3, ...), custom_call_target="tpu_custom_call" | custom-call | tf_op jit(solution)/shard_map/gate/pallas_call | solution.py:436
  (12 shorter events, 0.1 us)
Async XLA Ops:
  1.8 5.0 %collective-permute-start = (bf16[3,8,4096]{2,1,0:T(8,128)(2,1)S(1)}, bf16[3,8,4096]{2,1,0:T(8,128)(2,1)S(1)}, u32[]{:S(2)}, u32[]{:S(2)}) collective-permute-start(bf16[3,8,4096]{2,1,0:T(8,128)(2,1)S(1)} %pad_maximum_fusion), channel_id=1, source_target_pairs={{0,1},{1,2},{2,3},{3,4},{4,5},{5,6},{6,7},{7,8},{8,9},{9,10},{10,1... | collective-permute-start | bytes 589832 | tf_op jit(solution)/shard_map/ppermute | solution.py:319
  6.7 0.7 %copy-start.1 = (bf16[3,8,4096]{2,1,0:T(8,128)(2,1)}, bf16[3,8,4096]{2,1,0:T(8,128)(2,1)S(1)}, u32[]{:S(2)}) copy-start(bf16[3,8,4096]{2,1,0:T(8,128)(2,1)S(1)} %collective-permute-done.k_halo.v_halo.q_halo) | copy-start | bytes 589828
  7.4 25.8 %copy-start = (f32[8,16,2048]{2,1,0:T(8,128)S(1)}, f32[8,16,2048]{2,1,0:T(8,128)}, u32[]{:S(2)}) copy-start(f32[8,16,2048]{2,1,0:T(8,128)} %get-tuple-element.19) | copy-start | bytes 3145732
  7.4 27.5 %copy-start.4 = (f32[256,16]{0,1:T(8,128)S(1)}, f32[256,16]{0,1:T(8,128)}, u32[]{:S(2)}) copy-start(f32[256,16]{0,1:T(8,128)} %param.11) | copy-start | bytes 49156
  7.4 27.6 %copy-start.5 = (f32[256,16]{0,1:T(8,128)S(1)}, f32[256,16]{0,1:T(8,128)}, u32[]{:S(2)}) copy-start(f32[256,16]{0,1:T(8,128)} %param.12) | copy-start | bytes 49156
  26.5 6.8 %collective-permute-start.1 = (f32[16,4096]{1,0:T(8,128)}, f32[16,4096]{1,0:T(8,128)S(1)}, u32[]{:S(2)}, u32[]{:S(2)}) collective-permute-start(f32[16,4096]{1,0:T(8,128)} %get-tuple-element.20), channel_id=1, source_target_pairs={{0,1},{1,0},{2,3},{3,2},{4,5},{5,4},{6,7},{7,6},{8,9},{9,8},{10,11... | collective-permute-start | bytes 786440 | tf_op jit(solution)/shard_map/ppermute | solution.py:319
  34.2 4.4 %collective-permute-start.2 = (bf16[16,2048]{1,0:T(8,128)(2,1)S(1)}, bf16[16,2048]{1,0:T(8,128)(2,1)S(1)}, u32[]{:S(2)}, u32[]{:S(2)}) collective-permute-start(bf16[16,2048]{1,0:T(8,128)(2,1)S(1)} %get-tuple-element.27), channel_id=1, source_target_pairs={{0,2},{1,3},{2,0},{3,1},{4,6},{5,7},{6,4},{7,5},{8,10},{9,11},{10,... | collective-permute-start | bytes 196616 | tf_op jit(solution)/shard_map/ppermute | solution.py:319
  38.6 11.9 %copy-start.2 = (f32[16,4096]{1,0:T(8,128)S(1)}, f32[16,4096]{1,0:T(8,128)}, u32[]{:S(2)}) copy-start(f32[16,4096]{1,0:T(8,128)} %get-tuple-element.20) | copy-start | bytes 786436
  38.7 11.8 %collective-permute-start.5 = (bf16[16,2048]{1,0:T(8,128)(2,1)S(1)}, bf16[16,2048]{1,0:T(8,128)(2,1)S(1)}, u32[]{:S(2)}, u32[]{:S(2)}) collective-permute-start(bf16[16,2048]{1,0:T(8,128)(2,1)S(1)} %fusion.1), channel_id=1, source_target_pairs={{0,8},{1,9},{2,10},{3,11},{4,12},{5,13},{6,14},{7,15},{8,0},{9,1},... | collective-permute-start | bytes 196616 | tf_op jit(solution)/shard_map/ppermute | solution.py:319
  40.6 9.9 %collective-permute-start.4 = (bf16[16,2048]{1,0:T(8,128)(2,1)S(1)}, bf16[16,2048]{1,0:T(8,128)(2,1)S(1)}, u32[]{:S(2)}, u32[]{:S(2)}) collective-permute-start(bf16[16,2048]{1,0:T(8,128)(2,1)S(1)} %fusion.1), channel_id=1, source_target_pairs={{4,8},{5,9},{6,10},{7,11},{8,4},{9,5},{10,6},{11,7},{20,24},{21,25... | collective-permute-start | bytes 196616 | tf_op jit(solution)/shard_map/ppermute | solution.py:319
  41.3 9.2 %collective-permute-start.3 = (bf16[16,2048]{1,0:T(8,128)(2,1)S(1)}, bf16[16,2048]{1,0:T(8,128)(2,1)S(1)}, u32[]{:S(2)}, u32[]{:S(2)}) collective-permute-start(bf16[16,2048]{1,0:T(8,128)(2,1)S(1)} %fusion.1), channel_id=1, source_target_pairs={{0,4},{1,5},{2,6},{3,7},{4,0},{5,1},{6,2},{7,3},{8,12},{9,13},{10,... | collective-permute-start | bytes 196616 | tf_op jit(solution)/shard_map/ppermute | solution.py:319
  50.6 1.4 %collective-permute-start.6 = (f32[16,2048]{1,0:T(8,128)S(1)}, f32[16,2048]{1,0:T(8,128)S(1)}, u32[]{:S(2)}, u32[]{:S(2)}) collective-permute-start(f32[16,2048]{1,0:T(8,128)S(1)} %get-tuple-element.25), channel_id=1, source_target_pairs={{0,1},{1,0},{2,3},{3,2},{4,5},{5,4},{6,7},{7,6},{8,9},{9,8},{10,11... | collective-permute-start | bytes 393224 | tf_op jit(solution)/shard_map/ppermute | solution.py:319
  52.0 0.7 %copy-start.3 = (f32[16,2048]{1,0:T(8,128)}, f32[16,2048]{1,0:T(8,128)S(1)}, u32[]{:S(2)}) copy-start(f32[16,2048]{1,0:T(8,128)S(1)} %collective-permute-done.6.other_ref) | copy-start | bytes 393220

commit v4 on v3

--- a/solution.py
+++ b/solution.py
@@ -319,6 +319,10 @@
     return lax.ppermute(value, "ctx", pairs)
 
 
+def in_hbm(value):
+    return pltpu.with_memory_space_constraint(value, pltpu.HBM)
+
+
 def per_device(q_in, k_in, v_in, conv_filter, decay_rate, residue, genome_lengths):
     rows, width = q_in.shape
     tiles = width // LANES
@@ -334,7 +338,7 @@
     taps_spec = pl.BlockSpec((3, TAPS, block), lambda b, *_: (0, 0, b))
     row_spec = pl.BlockSpec((POLES, 8, LANES), lambda b, *_: (0, b, 0))
     local_spec = pl.BlockSpec((rows // 8, 8 * 8, LANES), lambda b, *_: (0, b, 0))
-    local_shape = jax.ShapeDtypeStruct((rows // 8, tiles * 8, LANES), F32)
+    local_shape = pltpu.HBM((rows // 8, tiles * 8, LANES), F32)
 
     def halo_spec(s):
         return pl.BlockSpec((1, 8, block), lambda b, *_: (s, 0, b))
@@ -355,8 +359,9 @@
         ],
         scratch_shapes=[pltpu.VMEM((POLES, width // 2), F32)],
         name="expand",
+        compiler_params=pltpu.CompilerParams(vmem_limit_bytes=16 << 20),
         cost_estimate=pl.CostEstimate(flops=10**9, bytes_accessed=10**6, transcendentals=0),
-    )(genome_lengths, decay_rate.T, residue.T)
+    )(genome_lengths, in_hbm(decay_rate.T), in_hbm(residue.T))
 
     local, span = pl.pallas_call(
         functools.partial(states_kernel, rows=rows, genomes=genomes),
@@ -375,7 +380,8 @@
         ),
         out_shape=[local_shape, jax.ShapeDtypeStruct((POLES, width), F32)],
         name="states",
-    )(relative, k_in, v_in, halo, halo, conv_filter, lam_rows, res_rows)
+        compiler_params=pltpu.CompilerParams(vmem_limit_bytes=40 << 20),
+    )(relative, k_in, v_in, halo, halo, in_hbm(conv_filter), lam_rows, res_rows)
 
     query = pl.pallas_call(
         functools.partial(query_kernel, rows=rows, genomes=genomes),
@@ -388,10 +394,11 @@
         ),
         out_shape=jax.ShapeDtypeStruct((rows, width), BF16),
         name="query",
+        compiler_params=pltpu.CompilerParams(vmem_limit_bytes=16 << 20),
         cost_estimate=pl.CostEstimate(
             flops=6 * 10**9, bytes_accessed=5 * rows * width, transcendentals=0
         ),
-    )(relative, q_in, halo, conv_filter)
+    )(relative, in_hbm(q_in), halo, in_hbm(conv_filter))
 
     core = index % 2
     half = width // 2
@@ -443,6 +450,7 @@
         ),
         out_shape=jax.ShapeDtypeStruct((rows, width), BF16),
         name="gate",
+        compiler_params=pltpu.CompilerParams(vmem_limit_bytes=40 << 20),
     )(
         relative, jnp.reshape(core, (1,)).astype(jnp.int32), local, query, mine, back,
         decay_rate.reshape(groups, 1, 2 * LANES), residue.reshape(groups, 1, 2 * LANES),

time: 60.5 us -> 55.9 us (0.924); the launches traced: 59.4 us -> 56 us
  Pallas kernels: 34.6 us -> 32.8 us
  local copies, waits for them, and re-layouts: 4.69 us -> 2.97 us
  other arithmetic: 1.77 us -> 0.27 us
  starting transfers between devices: 14.1 us -> 15.3 us
    pallas_call x1, Pallas kernels: 6.74 us -> 4.75 us  [per_device(): pl.pallas_call(functools.partial(gate_kernel, rows=rows, genomes=genomes)...]
    pallas_call x1, Pallas kernels: 19.1 us -> 20.5 us  [per_device(): pl.pallas_call(functools.partial(states_kernel, rows=rows, genomes=genome...]
    ppermute x7, starting transfers between devices: 14.1 us -> 15.3 us  [exchange(): return lax.ppermute(value, 'ctx', pairs)]
    convert_element_type x1, other arithmetic: 0.93 us -> 0.03 us  [per_device(): other = crossed(total.astype(BF16), size)]
    pallas_call x1, Pallas kernels: 2.53 us -> 1.7 us  [per_device(): pl.pallas_call(functools.partial(expand_kernel, tiles=tiles, count=count,...]
    unnamed x14, local copies, waits for them, and re-layouts: 1.54 us -> 0.88 us
    select_n x1, other arithmetic: 0.68 us -> 0.04 us  [per_device(): mine = jnp.where(core == 0, prefix, second)]
  transfers between devices with their start and end apart: 7 -> 7, of which waited for: 3 -> 3; matrix products, arithmetic and copies ran while one was open for 4% -> 1% of each run, Pallas kernels for 15% -> 14%
where the time goes in v4:
time: 55.9 us; the launch traced here: 56 us
  Pallas kernels  32.8 us (59%)
  starting transfers between devices  15.3 us (27%)
  waiting for transfers between devices  4.42 us (8%)
  local copies, waits for them, and re-layouts  2.97 us (5%)
    pallas_call x1, Pallas kernels, per_device(): pl.pallas_call(functools.partial(states_kernel, rows=rows, genomes=genome...  20.5 us
    ppermute x7, starting transfers between devices, exchange(): return lax.ppermute(value, 'ctx', pairs)  15.3 us
    pallas_call x1, Pallas kernels, per_device(): pl.pallas_call(functools.partial(query_kernel, rows=rows, genomes=genomes...  5.9 us
    pallas_call x1, Pallas kernels, per_device(): pl.pallas_call(functools.partial(gate_kernel, rows=rows, genomes=genomes)...  4.75 us
    ppermute x7, waiting for transfers between devices, exchange(): return lax.ppermute(value, 'ctx', pairs)  4.42 us
    another operation x2, local copies, waits for them, and re-layouts, per_device(): tail = jnp.stack([x[rows - 8:] for x in (q_in, k_in, v_in)])  1.87 us
    pallas_call x1, Pallas kernels, per_device(): pl.pallas_call(functools.partial(expand_kernel, tiles=tiles, count=count,...  1.7 us
  transfers between devices with their start and end apart: 7, of which 3 were waited for; matrix products, arithmetic and copies ran while one was open for 1% of the time, Pallas kernels for 14%

profile of v4, /device:TPU:0, one launch (start us, length us, event | category | flops | bytes accessed | tf_op | source)
XLA Modules:
  0.0 56.0 jit_solution(7903333964195856595)
XLA Ops:
  0.0 0.8 %slice_bitcast_fusion.2 = bf16[1,8,4096]{2,1,0:T(8,128)(2,1)S(1)} fusion(bf16[256,4096]{1,0:T(8,128)(2,1)} %q_ref.1), kind=kLoop, calls=%fused_computation.21 | loop fusion | bytes 131072 | tf_op jit(solution)/shard_map/stack | solution.py:332
  0.8 1.0 %slice_bitcast_fusion = (bf16[1,8,4096]{2,1,0:T(8,128)(2,1)S(1)}, bf16[1,8,4096]{2,1,0:T(8,128)(2,1)S(1)}) fusion(bf16[256,4096]{1,0:T(8,128)(2,1)} %v_ref.1, bf16[256,4096]{1,0:T(8,128)(2,1)} %k_ref.1), kind=kLoop, calls=%fused_computation.19 | loop fusion | bytes 262144 | tf_op jit(solution)/shard_map/stack | solution.py:332
  1.9 0.0 copy-start.1
  1.9 2.5 %collective-permute-start = (bf16[3,8,4096]{2,1,0:T(8,128)(2,1)S(1)}, bf16[3,8,4096]{2,1,0:T(8,128)(2,1)S(1)}, u32[]{:S(2)}, u32[]{:S(2)}) collective-permute-start(bf16[3,8,4096]{2,1,0:T(8,128)(2,1)S(1)} %pad_maximum_fusion), channel_id=1, source_target_pairs={{0,1},{1,2},{2,3},{3,4},{4,5},{5,6},{6,7},{7,8},{8,9},{9,10},{10,1... | collective-permute-start | bytes 589832 | tf_op jit(solution)/shard_map/ppermute | solution.py:319
  4.5 0.0 copy-start.3
  4.5 0.6 %copy-done.3 = s32[4]{0:T(128)S(1)} copy-done((s32[4]{0:T(128)S(1)}, s32[4]{0:T(128)}, u32[]{:S(2)}) %copy-start.3) | copy-done | bytes 40
  5.1 1.7 %expand.1 = (s32[4]{0:T(128)S(1)}, f32[16,32,128]{2,1,0:T(8,128)S(1)}, f32[16,32,128]{2,1,0:T(8,128)S(1)}, f32[8,16,2048]{2,1,0:T(8,128)S(1)}) custom-call(s32[4]{0:T(128)S(1)} %copy-done.3, f32[16,256]{1,0:T(8,128)} %bitcast.46, f32[16,256]{1,0:T(8,128)} %bitcast.47), custom_call_target="tpu_custom_call" | custom-call | flops 1000000000 | bytes 1000000 | tf_op jit(solution)/shard_map/expand/pallas_call | solution.py:350
  6.8 0.0 collective-permute-done.k_halo.v_halo.q_halo
  6.8 0.0 copy-done.2
  6.9 0.0 copy-done.1
  6.9 0.0 copy-start.4
  6.9 0.0 copy-start.5
  6.9 20.5 %states.1 = (f32[32,256,128]{2,1,0:T(8,128)}, f32[16,4096]{1,0:T(8,128)S(1)}) custom-call(s32[4]{0:T(128)S(1)} %get-tuple-element.15.starts, bf16[256,4096]{1,0:T(8,128)(2,1)S(1)} %copy-done.1, bf16[256,4096]{1,0:T(8,128)(2,1)S(1)} %copy-done.2, bf16[3,8,4096]{2,1,0:T(8,128)(2,1)S(1)} %collective-permute-done.k_halo.v_halo.q_halo, ...), custom_call_target="tpu_custom_call" | custom-call | tf_op jit(solution)/shard_map/states/pallas_call | solution.py:366
  27.4 1.0 %collective-permute-start.1 = (f32[16,4096]{1,0:T(8,128)S(1)}, f32[16,4096]{1,0:T(8,128)S(1)}, u32[]{:S(2)}, u32[]{:S(2)}) collective-permute-start(f32[16,4096]{1,0:T(8,128)S(1)} %get-tuple-element.20), channel_id=1, source_target_pairs={{0,1},{1,0},{2,3},{3,2},{4,5},{5,4},{6,7},{7,6},{8,9},{9,8},{10,11... | collective-permute-start | bytes 786440 | tf_op jit(solution)/shard_map/ppermute | solution.py:319
  28.4 1.2 %collective-permute-done.1 = f32[16,4096]{1,0:T(8,128)S(1)} collective-permute-done((f32[16,4096]{1,0:T(8,128)S(1)}, f32[16,4096]{1,0:T(8,128)S(1)}, u32[]{:S(2)}, u32[]{:S(2)}) %collective-permute-start.1) | collective-permute-done | bytes 262176 | tf_op jit(solution)/shard_map/ppermute | solution.py:319
  29.5 2.8 %collective-permute-start.2 = (bf16[16,2048]{1,0:T(8,128)(2,1)S(1)}, bf16[16,2048]{1,0:T(8,128)(2,1)S(1)}, u32[]{:S(2)}, u32[]{:S(2)}) collective-permute-start(bf16[16,2048]{1,0:T(8,128)(2,1)S(1)} %get-tuple-element.27), channel_id=1, source_target_pairs={{0,2},{1,3},{2,0},{3,1},{4,6},{5,7},{6,4},{7,5},{8,10},{9,11},{10,... | collective-permute-start | bytes 196616 | tf_op jit(solution)/shard_map/ppermute | solution.py:319
  32.4 0.1 copy.10
  32.5 0.1 copy.11
  32.6 0.1 reshape.12.lam_ref
  32.7 0.1 reshape.13.res_ref
  32.8 2.0 %collective-permute-done.2 = bf16[16,2048]{1,0:T(8,128)(2,1)S(1)} collective-permute-done((bf16[16,2048]{1,0:T(8,128)(2,1)S(1)}, bf16[16,2048]{1,0:T(8,128)(2,1)S(1)}, u32[]{:S(2)}, u32[]{:S(2)}) %collective-permute-start.2) | collective-permute-done | bytes 65568 | tf_op jit(solution)/shard_map/ppermute | solution.py:319
  34.8 5.7 %collective-permute-start.5 = (bf16[16,2048]{1,0:T(8,128)(2,1)S(1)}, bf16[16,2048]{1,0:T(8,128)(2,1)S(1)}, u32[]{:S(2)}, u32[]{:S(2)}) collective-permute-start(bf16[16,2048]{1,0:T(8,128)(2,1)S(1)} %fusion.1), channel_id=1, source_target_pairs={{0,8},{1,9},{2,10},{3,11},{4,12},{5,13},{6,14},{7,15},{8,0},{9,1},... | collective-permute-start | bytes 196616 | tf_op jit(solution)/shard_map/ppermute | solution.py:319
  40.5 0.7 %collective-permute-start.4 = (bf16[16,2048]{1,0:T(8,128)(2,1)S(1)}, bf16[16,2048]{1,0:T(8,128)(2,1)S(1)}, u32[]{:S(2)}, u32[]{:S(2)}) collective-permute-start(bf16[16,2048]{1,0:T(8,128)(2,1)S(1)} %fusion.1), channel_id=1, source_target_pairs={{4,8},{5,9},{6,10},{7,11},{8,4},{9,5},{10,6},{11,7},{20,24},{21,25... | collective-permute-start | bytes 196616 | tf_op jit(solution)/shard_map/ppermute | solution.py:319
  41.2 2.5 %collective-permute-start.3 = (bf16[16,2048]{1,0:T(8,128)(2,1)S(1)}, bf16[16,2048]{1,0:T(8,128)(2,1)S(1)}, u32[]{:S(2)}, u32[]{:S(2)}) collective-permute-start(bf16[16,2048]{1,0:T(8,128)(2,1)S(1)} %fusion.1), channel_id=1, source_target_pairs={{0,4},{1,5},{2,6},{3,7},{4,0},{5,1},{6,2},{7,3},{8,12},{9,13},{10,... | collective-permute-start | bytes 196616 | tf_op jit(solution)/shard_map/ppermute | solution.py:319
  43.7 5.9 %query.1.query_ref = bf16[256,4096]{1,0:T(8,128)(2,1)S(1)} custom-call(s32[4]{0:T(128)S(1)} %get-tuple-element.15.starts, bf16[256,4096]{1,0:T(8,128)(2,1)} %q_ref.1, bf16[3,8,4096]{2,1,0:T(8,128)(2,1)S(1)} %collective-permute-done.k_halo.v_halo.q_halo, f32[3,7,4096]{2,1,0:T(8,128)} %taps_ref.3), custom_call_target="tpu_custom_call" | custom-call | flops 6000000000 | bytes 5242880 | tf_op jit(solution)/shard_map/query/pallas_call | solution.py:386
  49.6 0.0 collective-permute-done.5
  49.7 0.0 collective-permute-done.4
  49.7 0.0 collective-permute-done.3
  49.7 0.1 fusion.7
  49.8 0.1 collective-permute-start.6
  50.0 1.3 %collective-permute-done.6.other_ref = f32[16,2048]{1,0:T(8,128)S(1)} collective-permute-done((f32[16,2048]{1,0:T(8,128)S(1)}, f32[16,2048]{1,0:T(8,128)S(1)}, u32[]{:S(2)}, u32[]{:S(2)}) %collective-permute-start.6) | collective-permute-done | bytes 131104 | tf_op jit(solution)/shard_map/ppermute | solution.py:319
  51.2 4.7 %gate.1 = bf16[256,4096]{1,0:T(8,128)(2,1)} custom-call(s32[4]{0:T(128)S(1)} %get-tuple-element.15.starts, s32[1]{0:T(128)} %bitcast.2.core_ref, f32[32,256,128]{2,1,0:T(8,128)S(1)} %copy-done, bf16[256,4096]{1,0:T(8,128)(2,1)S(1)} %query.1.query_ref, f32[16,2048]{1,0:T(8,128)S(1)} %fusion.8.mine_ref, f32[16,2048]{1,0:T(8,128)S(1)} %collective-permute-done.6.other_ref, ...), custom_call_target="tpu_custom_call" | custom-call | tf_op jit(solution)/shard_map/gate/pallas_call | solution.py:443
  (12 shorter events, 0.2 us)
Async XLA Ops:
  0.8 6.0 %copy-start.2 = (bf16[256,4096]{1,0:T(8,128)(2,1)S(1)}, bf16[256,4096]{1,0:T(8,128)(2,1)}, u32[]{:S(2)}) copy-start(bf16[256,4096]{1,0:T(8,128)(2,1)} %v_ref.1) | copy-start | bytes 6291460
  1.9 5.0 %copy-start.1 = (bf16[256,4096]{1,0:T(8,128)(2,1)S(1)}, bf16[256,4096]{1,0:T(8,128)(2,1)}, u32[]{:S(2)}) copy-start(bf16[256,4096]{1,0:T(8,128)(2,1)} %k_ref.1) | copy-start | bytes 6291460
  1.9 4.9 %collective-permute-start = (bf16[3,8,4096]{2,1,0:T(8,128)(2,1)S(1)}, bf16[3,8,4096]{2,1,0:T(8,128)(2,1)S(1)}, u32[]{:S(2)}, u32[]{:S(2)}) collective-permute-start(bf16[3,8,4096]{2,1,0:T(8,128)(2,1)S(1)} %pad_maximum_fusion), channel_id=1, source_target_pairs={{0,1},{1,2},{2,3},{3,4},{4,5},{5,6},{6,7},{7,8},{8,9},{9,10},{10,1... | collective-permute-start | bytes 589832 | tf_op jit(solution)/shard_map/ppermute | solution.py:319
  4.5 0.7 %copy-start.3 = (s32[4]{0:T(128)S(1)}, s32[4]{0:T(128)}, u32[]{:S(2)}) copy-start(s32[4]{0:T(128)} %lengths.1) | copy-start | bytes 52
  6.9 25.5 %copy-start.4 = (f32[256,16]{0,1:T(8,128)S(1)}, f32[256,16]{0,1:T(8,128)}, u32[]{:S(2)}) copy-start(f32[256,16]{0,1:T(8,128)} %param.11) | copy-start | bytes 49156
  6.9 25.6 %copy-start.5 = (f32[256,16]{0,1:T(8,128)S(1)}, f32[256,16]{0,1:T(8,128)}, u32[]{:S(2)}) copy-start(f32[256,16]{0,1:T(8,128)} %param.12) | copy-start | bytes 49156
  27.4 2.1 %collective-permute-start.1 = (f32[16,4096]{1,0:T(8,128)S(1)}, f32[16,4096]{1,0:T(8,128)S(1)}, u32[]{:S(2)}, u32[]{:S(2)}) collective-permute-start(f32[16,4096]{1,0:T(8,128)S(1)} %get-tuple-element.20), channel_id=1, source_target_pairs={{0,1},{1,0},{2,3},{3,2},{4,5},{5,4},{6,7},{7,6},{8,9},{9,8},{10,11... | collective-permute-start | bytes 786440 | tf_op jit(solution)/shard_map/ppermute | solution.py:319
  29.5 5.2 %collective-permute-start.2 = (bf16[16,2048]{1,0:T(8,128)(2,1)S(1)}, bf16[16,2048]{1,0:T(8,128)(2,1)S(1)}, u32[]{:S(2)}, u32[]{:S(2)}) collective-permute-start(bf16[16,2048]{1,0:T(8,128)(2,1)S(1)} %get-tuple-element.27), channel_id=1, source_target_pairs={{0,2},{1,3},{2,0},{3,1},{4,6},{5,7},{6,4},{7,5},{8,10},{9,11},{10,... | collective-permute-start | bytes 196616 | tf_op jit(solution)/shard_map/ppermute | solution.py:319
  34.8 14.8 %collective-permute-start.5 = (bf16[16,2048]{1,0:T(8,128)(2,1)S(1)}, bf16[16,2048]{1,0:T(8,128)(2,1)S(1)}, u32[]{:S(2)}, u32[]{:S(2)}) collective-permute-start(bf16[16,2048]{1,0:T(8,128)(2,1)S(1)} %fusion.1), channel_id=1, source_target_pairs={{0,8},{1,9},{2,10},{3,11},{4,12},{5,13},{6,14},{7,15},{8,0},{9,1},... | collective-permute-start | bytes 196616 | tf_op jit(solution)/shard_map/ppermute | solution.py:319
  40.5 9.2 %collective-permute-start.4 = (bf16[16,2048]{1,0:T(8,128)(2,1)S(1)}, bf16[16,2048]{1,0:T(8,128)(2,1)S(1)}, u32[]{:S(2)}, u32[]{:S(2)}) collective-permute-start(bf16[16,2048]{1,0:T(8,128)(2,1)S(1)} %fusion.1), channel_id=1, source_target_pairs={{4,8},{5,9},{6,10},{7,11},{8,4},{9,5},{10,6},{11,7},{20,24},{21,25... | collective-permute-start | bytes 196616 | tf_op jit(solution)/shard_map/ppermute | solution.py:319
  41.2 8.5 %collective-permute-start.3 = (bf16[16,2048]{1,0:T(8,128)(2,1)S(1)}, bf16[16,2048]{1,0:T(8,128)(2,1)S(1)}, u32[]{:S(2)}, u32[]{:S(2)}) collective-permute-start(bf16[16,2048]{1,0:T(8,128)(2,1)S(1)} %fusion.1), channel_id=1, source_target_pairs={{0,4},{1,5},{2,6},{3,7},{4,0},{5,1},{6,2},{7,3},{8,12},{9,13},{10,... | collective-permute-start | bytes 196616 | tf_op jit(solution)/shard_map/ppermute | solution.py:319
  43.7 7.5 %copy-start = (f32[32,256,128]{2,1,0:T(8,128)S(1)}, f32[32,256,128]{2,1,0:T(8,128)}, u32[]{:S(2)}) copy-start(f32[32,256,128]{2,1,0:T(8,128)} %get-tuple-element.18.local_ref) | copy-start | bytes 12582916
  49.8 1.4 %collective-permute-start.6 = (f32[16,2048]{1,0:T(8,128)S(1)}, f32[16,2048]{1,0:T(8,128)S(1)}, u32[]{:S(2)}, u32[]{:S(2)}) collective-permute-start(f32[16,2048]{1,0:T(8,128)S(1)} %get-tuple-element.25), channel_id=1, source_target_pairs={{0,1},{1,0},{2,3},{3,2},{4,5},{5,4},{6,7},{7,6},{8,9},{9,8},{10,11... | collective-permute-start | bytes 393224 | tf_op jit(solution)/shard_map/ppermute | solution.py:319

commit v5 on v4

--- a/solution.py
+++ b/solution.py
@@ -124,9 +124,6 @@
     return sizes, size if size * 4 == count else 0
 
 
-FLIPS = (1, 3, 2)
-
-
 def factors(lengths, index, count, rows, genomes):
     starts = [jnp.int32(0)]
     for g in range(1, genomes):
@@ -151,13 +148,14 @@
         out.append((jnp.where(right, 0, size), jnp.where(right, 1.0, joined(last, last + size))))
     if wide:
         block = lax.div(index, wide)
-        for flip in FLIPS:
-            source = block ^ flip
+        for source in (block - 1, block ^ 2):
             after = (source + 1) * wide
             out.append(
                 (
                     jnp.maximum(chip - after, 0),
-                    jnp.where(source < block, joined(after - 1, chip - 1), 0.0),
+                    jnp.where(
+                        (source >= 0) & (source < block), joined(after - 1, chip - 1), 0.0
+                    ),
                 )
             )
     out.append((jnp.int32(1), joined(chip - 1, chip)))
@@ -205,6 +203,11 @@
         factor_ref[i] = factor * jnp.exp(-lam_mine[...] * (devices * rows).astype(F32))
 
 
+def tail_kernel(q_ref, k_ref, v_ref, out_ref):
+    for s, ref in enumerate((q_ref, k_ref, v_ref)):
+        out_ref[s] = ref[...]
+
+
 def states_kernel(
     starts, k_ref, v_ref, k_halo, v_halo, taps_ref, lam_ref, res_ref,
     local_ref, span_ref, xs, mixed, final, *, rows, genomes,
@@ -329,7 +332,15 @@
     genomes = genome_lengths.shape[0]
     count = lax.axis_size("ctx")
     index = lax.axis_index("ctx")
-    tail = jnp.stack([x[rows - 8 :] for x in (q_in, k_in, v_in)])
+    tail = pl.pallas_call(
+        tail_kernel,
+        grid=(1,),
+        in_specs=[pl.BlockSpec((8, width), lambda i: (rows // 8 - 1, 0))] * 3,
+        out_specs=pl.BlockSpec((3, 8, width), lambda i: (0, 0, 0)),
+        out_shape=jax.ShapeDtypeStruct((3, 8, width), BF16),
+        name="tail",
+        compiler_params=pltpu.CompilerParams(vmem_limit_bytes=16 << 20),
+    )(in_hbm(q_in), in_hbm(k_in), in_hbm(v_in))
     halo = exchange(tail, [(i, i + 1) for i in range(count - 1)])
 
     block = 8 * LANES
@@ -346,7 +357,7 @@
     in_smem = pl.BlockSpec(memory_space=pltpu.SMEM)
     in_vmem = pl.BlockSpec(memory_space=pltpu.VMEM)
     sizes, wide = exchange_plan(count)
-    terms = 2 + 3 * len(sizes) + (len(FLIPS) if wide else 0)
+    terms = 2 + 3 * len(sizes) + (2 if wide else 0)
     relative, lam_rows, res_rows, factor = pl.pallas_call(
         functools.partial(expand_kernel, tiles=tiles, count=count, rows=rows, genomes=genomes),
         in_specs=[in_smem, in_vmem, in_vmem],
@@ -361,7 +372,7 @@
         name="expand",
         compiler_params=pltpu.CompilerParams(vmem_limit_bytes=16 << 20),
         cost_estimate=pl.CostEstimate(flops=10**9, bytes_accessed=10**6, transcendentals=0),
-    )(genome_lengths, in_hbm(decay_rate.T), in_hbm(residue.T))
+    )(in_hbm(genome_lengths), in_hbm(decay_rate.T), in_hbm(residue.T))
 
     local, span = pl.pallas_call(
         functools.partial(states_kernel, rows=rows, genomes=genomes),
@@ -409,9 +420,8 @@
     def term(i, value):
         return factor[i] * value
 
-    def crossed(value, step, only=None):
-        pairs = [(i, i ^ step) for i in range(count) if only is None or i // only % 4 in (1, 2)]
-        return exchange(value, pairs).astype(F32)
+    def crossed(value, step):
+        return exchange(value, [(i, i ^ step) for i in range(count)]).astype(F32)
 
     own = mine_of(span)
     got = mine_of(exchange(span, [(i, i ^ 1) for i in range(count)]))
@@ -427,7 +437,10 @@
         at += 3
     if wide:
         sent = total.astype(BF16)
-        others = [crossed(sent, f * wide, wide if f == 3 else None) for f in FLIPS]
+        others = [
+            exchange(sent, [(i, i + wide) for i in range(count - wide)]).astype(F32),
+            crossed(sent, 2 * wide),
+        ]
         query, *others = lax.optimization_barrier((query, *others))
         for other in others:
             prefix = prefix + term(at, other)

time: 55.9 us -> 54.7 us (0.979)
  local copies, waits for them, and re-layouts: 2.97 us -> 0.44 us
  starting transfers between devices: 15.3 us -> 17.7 us
  Pallas kernels: 32.8 us -> 31.7 us
    ppermute x7 -> x6, starting transfers between devices: 15.3 us -> 17.7 us  [exchange(): return lax.ppermute(value, 'ctx', pairs)]
    another operation x2 -> x0, local copies, waits for them, and re-layouts: 1.87 us -> none  [per_device(): tail = jnp.stack([x[rows - 8:] for x in (q_in, k_in, v_in)])]
    pallas_call x1, Pallas kernels: 20.5 us -> 18.7 us  [per_device(): pl.pallas_call(functools.partial(states_kernel, rows=rows, genomes=genome...]
    pallas_call x0 -> x1, Pallas kernels: none -> 1.06 us  [per_device(): pl.pallas_call(tail_kernel, grid=(1,), in_specs=[pl.BlockSpec((8, width),...]
    unnamed x14 -> x12, local copies, waits for them, and re-layouts: 0.88 us -> 0.23 us
    ppermute x7 -> x6, waiting for transfers between devices: 4.42 us -> 4.42 us  [exchange(): return lax.ppermute(value, 'ctx', pairs)]
  transfers between devices with their start and end apart: 7 -> 6, of which waited for: 3 -> 3; matrix products, arithmetic and copies ran while one was open for 1% -> 1% of each run, Pallas kernels for 14% -> 13%
where the time goes in v5:
time: 54.7 us; the launch traced here: 54.6 us
  Pallas kernels  31.7 us (58%)
  starting transfers between devices  17.7 us (32%)
  waiting for transfers between devices  4.42 us (8%)
    pallas_call x1, Pallas kernels, per_device(): pl.pallas_call(functools.partial(states_kernel, rows=rows, genomes=genome...  18.7 us
    ppermute x6, starting transfers between devices, exchange(): return lax.ppermute(value, 'ctx', pairs)  17.7 us
    pallas_call x1, Pallas kernels, per_device(): pl.pallas_call(functools.partial(query_kernel, rows=rows, genomes=genomes...  5.49 us
    pallas_call x1, Pallas kernels, per_device(): pl.pallas_call(functools.partial(gate_kernel, rows=rows, genomes=genomes)...  4.75 us
    ppermute x6, waiting for transfers between devices, exchange(): return lax.ppermute(value, 'ctx', pairs)  4.42 us
    pallas_call x1, Pallas kernels, per_device(): pl.pallas_call(functools.partial(expand_kernel, tiles=tiles, count=count,...  1.7 us
  transfers between devices with their start and end apart: 6, of which 3 were waited for; matrix products, arithmetic and copies ran while one was open for 1% of the time, Pallas kernels for 13%

profile of v5, /device:TPU:0, one launch (start us, length us, event | category | flops | bytes accessed | tf_op | source)
XLA Modules:
  0.0 54.6 jit_solution(10328066114787635813)
XLA Ops:
  0.0 0.0 copy-start.1
  0.0 1.1 %tail.1 = bf16[3,8,4096]{2,1,0:T(8,128)(2,1)S(1)} custom-call(bf16[256,4096]{1,0:T(8,128)(2,1)} %q_ref.3, bf16[256,4096]{1,0:T(8,128)(2,1)} %k_ref.3, bf16[256,4096]{1,0:T(8,128)(2,1)} %v_ref.3), custom_call_target="tpu_custom_call" | custom-call | tf_op jit(solution)/shard_map/tail/pallas_call | solution.py:335
  1.1 0.0 copy-start
  1.1 2.5 %collective-permute-start = (bf16[3,8,4096]{2,1,0:T(8,128)(2,1)S(1)}, bf16[3,8,4096]{2,1,0:T(8,128)(2,1)S(1)}, u32[]{:S(2)}, u32[]{:S(2)}) collective-permute-start(bf16[3,8,4096]{2,1,0:T(8,128)(2,1)S(1)} %tail.1), channel_id=1, source_target_pairs={{0,1},{1,2},{2,3},{3,4},{4,5},{5,6},{6,7},{7,8},{8,9},{9,10},{10,1... | collective-permute-start | bytes 589832 | tf_op jit(solution)/shard_map/ppermute | solution.py:322
  3.6 1.7 %expand.1 = (s32[4]{0:T(128)S(1)}, f32[16,32,128]{2,1,0:T(8,128)S(1)}, f32[16,32,128]{2,1,0:T(8,128)S(1)}, f32[7,16,2048]{2,1,0:T(8,128)S(1)}) custom-call(s32[4]{0:T(128)} %lengths.1, f32[16,256]{1,0:T(8,128)} %bitcast.35, f32[16,256]{1,0:T(8,128)} %bitcast.36), custom_call_target="tpu_custom_call" | custom-call | flops 1000000000 | bytes 1000000 | tf_op jit(solution)/shard_map/expand/pallas_call | solution.py:361
  5.3 0.0 collective-permute-done.k_halo.v_halo.q_halo
  5.3 0.0 copy-done.1
  5.4 0.0 copy-done
  5.4 0.0 copy-start.3
  5.4 0.0 copy-start.4
  5.4 18.7 %states.1 = (f32[32,256,128]{2,1,0:T(8,128)}, f32[16,4096]{1,0:T(8,128)S(1)}) custom-call(s32[4]{0:T(128)S(1)} %get-tuple-element.14.starts, bf16[256,4096]{1,0:T(8,128)(2,1)S(1)} %copy-done, bf16[256,4096]{1,0:T(8,128)(2,1)S(1)} %copy-done.1, bf16[3,8,4096]{2,1,0:T(8,128)(2,1)S(1)} %collective-permute-done.k_halo.v_halo.q_halo, ...), custom_call_target="tpu_custom_call" | custom-call | tf_op jit(solution)/shard_map/states/pallas_call | solution.py:377
  24.1 3.5 %collective-permute-start.1 = (f32[16,4096]{1,0:T(8,128)S(1)}, f32[16,4096]{1,0:T(8,128)S(1)}, u32[]{:S(2)}, u32[]{:S(2)}) collective-permute-start(f32[16,4096]{1,0:T(8,128)S(1)} %get-tuple-element.19), channel_id=1, source_target_pairs={{0,1},{1,0},{2,3},{3,2},{4,5},{5,4},{6,7},{7,6},{8,9},{9,8},{10,11... | collective-permute-start | bytes 786440 | tf_op jit(solution)/shard_map/ppermute | solution.py:322
  27.5 1.2 %collective-permute-done.1 = f32[16,4096]{1,0:T(8,128)S(1)} collective-permute-done((f32[16,4096]{1,0:T(8,128)S(1)}, f32[16,4096]{1,0:T(8,128)S(1)}, u32[]{:S(2)}, u32[]{:S(2)}) %collective-permute-start.1) | collective-permute-done | bytes 262176 | tf_op jit(solution)/shard_map/ppermute | solution.py:322
  28.7 2.8 %collective-permute-start.2 = (bf16[16,2048]{1,0:T(8,128)(2,1)S(1)}, bf16[16,2048]{1,0:T(8,128)(2,1)S(1)}, u32[]{:S(2)}, u32[]{:S(2)}) collective-permute-start(bf16[16,2048]{1,0:T(8,128)(2,1)S(1)} %get-tuple-element.25), channel_id=1, source_target_pairs={{0,2},{1,3},{2,0},{3,1},{4,6},{5,7},{6,4},{7,5},{8,10},{9,11},{10,... | collective-permute-start | bytes 196616 | tf_op jit(solution)/shard_map/ppermute | solution.py:322
  31.5 0.0 copy-done.3
  31.5 0.1 copy.10
  31.6 0.0 copy-done.4
  31.6 0.1 copy.11
  31.7 0.1 reshape.12.lam_ref
  31.9 0.1 reshape.13.res_ref
  32.0 2.0 %collective-permute-done.2 = bf16[16,2048]{1,0:T(8,128)(2,1)S(1)} collective-permute-done((bf16[16,2048]{1,0:T(8,128)(2,1)S(1)}, bf16[16,2048]{1,0:T(8,128)(2,1)S(1)}, u32[]{:S(2)}, u32[]{:S(2)}) %collective-permute-start.2) | collective-permute-done | bytes 65568 | tf_op jit(solution)/shard_map/ppermute | solution.py:322
  34.0 3.9 %collective-permute-start.4 = (bf16[16,2048]{1,0:T(8,128)(2,1)S(1)}, bf16[16,2048]{1,0:T(8,128)(2,1)S(1)}, u32[]{:S(2)}, u32[]{:S(2)}) collective-permute-start(bf16[16,2048]{1,0:T(8,128)(2,1)S(1)} %fusion.1), channel_id=1, source_target_pairs={{0,8},{1,9},{2,10},{3,11},{4,12},{5,13},{6,14},{7,15},{8,0},{9,1},... | collective-permute-start | bytes 196616 | tf_op jit(solution)/shard_map/ppermute | solution.py:322
  37.9 4.9 %collective-permute-start.3 = (bf16[16,2048]{1,0:T(8,128)(2,1)S(1)}, bf16[16,2048]{1,0:T(8,128)(2,1)S(1)}, u32[]{:S(2)}, u32[]{:S(2)}) collective-permute-start(bf16[16,2048]{1,0:T(8,128)(2,1)S(1)} %fusion.1), channel_id=1, source_target_pairs={{0,4},{1,5},{2,6},{3,7},{4,8},{5,9},{6,10},{7,11},{8,12},{9,13},{1... | collective-permute-start | bytes 196616 | tf_op jit(solution)/shard_map/ppermute | solution.py:322
  42.8 0.0 copy-start.2
  42.8 5.5 %query.1.query_ref = bf16[256,4096]{1,0:T(8,128)(2,1)S(1)} custom-call(s32[4]{0:T(128)S(1)} %get-tuple-element.14.starts, bf16[256,4096]{1,0:T(8,128)(2,1)} %q_ref.3, bf16[3,8,4096]{2,1,0:T(8,128)(2,1)S(1)} %collective-permute-done.k_halo.v_halo.q_halo, f32[3,7,4096]{2,1,0:T(8,128)} %taps_ref.3), custom_call_target="tpu_custom_call" | custom-call | flops 6000000000 | bytes 5242880 | tf_op jit(solution)/shard_map/query/pallas_call | solution.py:397
  48.3 0.0 collective-permute-done.4
  48.4 0.0 collective-permute-done.3
  48.4 0.1 fusion.6
  48.5 0.1 collective-permute-start.5
  48.6 1.3 %collective-permute-done.5.other_ref = f32[16,2048]{1,0:T(8,128)S(1)} collective-permute-done((f32[16,2048]{1,0:T(8,128)S(1)}, f32[16,2048]{1,0:T(8,128)S(1)}, u32[]{:S(2)}, u32[]{:S(2)}) %collective-permute-start.5) | collective-permute-done | bytes 131104 | tf_op jit(solution)/shard_map/ppermute | solution.py:322
  49.9 0.0 copy-done.2
  49.9 4.7 %gate.1 = bf16[256,4096]{1,0:T(8,128)(2,1)} custom-call(s32[4]{0:T(128)S(1)} %get-tuple-element.14.starts, s32[1]{0:T(128)} %bitcast.2.core_ref, f32[32,256,128]{2,1,0:T(8,128)S(1)} %copy-done.2, bf16[256,4096]{1,0:T(8,128)(2,1)S(1)} %query.1.query_ref, f32[16,2048]{1,0:T(8,128)S(1)} %fusion.7.mine_ref, f32[16,2048]{1,0:T(8,128)S(1)} %collective-permute-done.5.other_ref, ...), custom_call_target="tpu_custom_call" | custom-call | tf_op jit(solution)/shard_map/gate/pallas_call | solution.py:456
  (5 shorter events, 0.1 us)
Async XLA Ops:
  0.0 5.4 %copy-start.1 = (bf16[256,4096]{1,0:T(8,128)(2,1)S(1)}, bf16[256,4096]{1,0:T(8,128)(2,1)}, u32[]{:S(2)}) copy-start(bf16[256,4096]{1,0:T(8,128)(2,1)} %v_ref.3) | copy-start | bytes 6291460
  1.1 4.3 %copy-start = (bf16[256,4096]{1,0:T(8,128)(2,1)S(1)}, bf16[256,4096]{1,0:T(8,128)(2,1)}, u32[]{:S(2)}) copy-start(bf16[256,4096]{1,0:T(8,128)(2,1)} %k_ref.3) | copy-start | bytes 6291460
  1.1 4.3 %collective-permute-start = (bf16[3,8,4096]{2,1,0:T(8,128)(2,1)S(1)}, bf16[3,8,4096]{2,1,0:T(8,128)(2,1)S(1)}, u32[]{:S(2)}, u32[]{:S(2)}) collective-permute-start(bf16[3,8,4096]{2,1,0:T(8,128)(2,1)S(1)} %tail.1), channel_id=1, source_target_pairs={{0,1},{1,2},{2,3},{3,4},{4,5},{5,6},{6,7},{7,8},{8,9},{9,10},{10,1... | collective-permute-start | bytes 589832 | tf_op jit(solution)/shard_map/ppermute | solution.py:322
  5.4 26.2 %copy-start.3 = (f32[256,16]{0,1:T(8,128)S(1)}, f32[256,16]{0,1:T(8,128)}, u32[]{:S(2)}) copy-start(f32[256,16]{0,1:T(8,128)} %param.11) | copy-start | bytes 49156
  5.4 26.3 %copy-start.4 = (f32[256,16]{0,1:T(8,128)S(1)}, f32[256,16]{0,1:T(8,128)}, u32[]{:S(2)}) copy-start(f32[256,16]{0,1:T(8,128)} %param.12) | copy-start | bytes 49156
  24.1 4.6 %collective-permute-start.1 = (f32[16,4096]{1,0:T(8,128)S(1)}, f32[16,4096]{1,0:T(8,128)S(1)}, u32[]{:S(2)}, u32[]{:S(2)}) collective-permute-start(f32[16,4096]{1,0:T(8,128)S(1)} %get-tuple-element.19), channel_id=1, source_target_pairs={{0,1},{1,0},{2,3},{3,2},{4,5},{5,4},{6,7},{7,6},{8,9},{9,8},{10,11... | collective-permute-start | bytes 786440 | tf_op jit(solution)/shard_map/ppermute | solution.py:322
  28.7 5.2 %collective-permute-start.2 = (bf16[16,2048]{1,0:T(8,128)(2,1)S(1)}, bf16[16,2048]{1,0:T(8,128)(2,1)S(1)}, u32[]{:S(2)}, u32[]{:S(2)}) collective-permute-start(bf16[16,2048]{1,0:T(8,128)(2,1)S(1)} %get-tuple-element.25), channel_id=1, source_target_pairs={{0,2},{1,3},{2,0},{3,1},{4,6},{5,7},{6,4},{7,5},{8,10},{9,11},{10,... | collective-permute-start | bytes 196616 | tf_op jit(solution)/shard_map/ppermute | solution.py:322
  34.0 14.4 %collective-permute-start.4 = (bf16[16,2048]{1,0:T(8,128)(2,1)S(1)}, bf16[16,2048]{1,0:T(8,128)(2,1)S(1)}, u32[]{:S(2)}, u32[]{:S(2)}) collective-permute-start(bf16[16,2048]{1,0:T(8,128)(2,1)S(1)} %fusion.1), channel_id=1, source_target_pairs={{0,8},{1,9},{2,10},{3,11},{4,12},{5,13},{6,14},{7,15},{8,0},{9,1},... | collective-permute-start | bytes 196616 | tf_op jit(solution)/shard_map/ppermute | solution.py:322
  37.9 10.5 %collective-permute-start.3 = (bf16[16,2048]{1,0:T(8,128)(2,1)S(1)}, bf16[16,2048]{1,0:T(8,128)(2,1)S(1)}, u32[]{:S(2)}, u32[]{:S(2)}) collective-permute-start(bf16[16,2048]{1,0:T(8,128)(2,1)S(1)} %fusion.1), channel_id=1, source_target_pairs={{0,4},{1,5},{2,6},{3,7},{4,8},{5,9},{6,10},{7,11},{8,12},{9,13},{1... | collective-permute-start | bytes 196616 | tf_op jit(solution)/shard_map/ppermute | solution.py:322
  42.8 7.1 %copy-start.2 = (f32[32,256,128]{2,1,0:T(8,128)S(1)}, f32[32,256,128]{2,1,0:T(8,128)}, u32[]{:S(2)}) copy-start(f32[32,256,128]{2,1,0:T(8,128)} %get-tuple-element.17.local_ref) | copy-start | bytes 12582916
  48.5 1.4 %collective-permute-start.5 = (f32[16,2048]{1,0:T(8,128)S(1)}, f32[16,2048]{1,0:T(8,128)S(1)}, u32[]{:S(2)}, u32[]{:S(2)}) collective-permute-start(f32[16,2048]{1,0:T(8,128)S(1)} %get-tuple-element.23), channel_id=1, source_target_pairs={{0,1},{1,0},{2,3},{3,2},{4,5},{5,4},{6,7},{7,6},{8,9},{9,8},{10,11... | collective-permute-start | bytes 393224 | tf_op jit(solution)/shard_map/ppermute | solution.py:322
